TPU v7x, 32 devices: a whole 2x2x4 slice. The times are simulated.
32 devices in a mesh: groups: 2 (over y), store: 8 (over z, x), tensor: 2 (over core).
Axes of the slice: x: 2, y: 2, z: 4, core: 2. Of those that a mesh axis runs over, the one named last changes fastest.
Arguments:
- queries: bfloat16 [32, 8192], P(('groups', 'store'), 'tensor'), parts along dimension 0, may hold values from -200 to 200
- new_kv: bfloat16 [32, 2, 1024], P(('groups', 'store'), None, 'tensor'), parts along dimension 0, may hold values from -15 to 15
- kv_pages: bfloat16 [128, 2, 256, 1024], P(('groups', 'store'), None, None, 'tensor'), parts along dimension 0, may hold values from -15 to 15
- page_index: int32 [32, 4], P(('groups', 'store')), parts along dimension 0, may hold values from 0 to 7
- page_owner: int32 [32, 4], P(('groups', 'store')), parts along dimension 0, may hold values from 0 to 7, as said below
- seq_pages: int32 [32], P(('groups', 'store')), parts along dimension 0, may hold values from 1 to 4, as said below
Outputs:
- attended: bfloat16 [32, 8192], P(('groups', 'store'), 'tensor'), parts along dimension 0
There are 2 independent parts, one for each index of `groups`. A program takes and returns all parts, laid end to end along the dimension named above; each array names one. Nothing has to cross between parts.
Inputs may be any that keep to these rules, and one draw needn't show every extreme that they name: `page_owner`: page j of sequence s lies on store index (s // 2 + o) modulo the number of store indices, with o from 0 to 3; over the slots of the sequences of one store index, at most 2 share one o, so at most 2 live pages of those sequences lie on one store index. `seq_pages`: the sequences of store index 0 all have 4 pages.
All inputs are finite; a program needn't handle non-finite values.
Results may differ from a plain program's by a relative error of at most 0.0011.
Values may be sent and summed in bfloat16 or wider, within the bound.
No kernel may reach another device: no remote copies, remote signals or barrier semaphores. Data moves between devices by JAX's collectives and lax.ppermute only.
A program may use at most 64 MiB of HBM per device.

v0:
```python
import jax
import jax.numpy as jnp
from jax import lax
from jax.sharding import PartitionSpec as P

HEAD_DIM = 128
REACH = 4


def shifted(value, axis, steps):
    count = lax.axis_size(axis)
    pairs = [(source, (source + steps) % count) for source in range(count)]
    return lax.ppermute(value, axis, pairs)


def page_partial(query_rows, served, scale):
    slots, _, length, width = served.shape
    kv_count = query_rows.shape[1]
    keys = served[:, 0].reshape(slots, length, kv_count, width // kv_count)
    values = served[:, 1].reshape(slots, length, kv_count, width // kv_count)
    scores = (
        jnp.einsum("ckgd,cpkd->ckgp", query_rows, keys, preferred_element_type=jnp.float32) * scale
    )
    peak = jnp.max(scores, axis=-1)
    weights = jnp.exp(scores - peak[..., None])
    total = jnp.sum(weights, axis=-1)
    summed = jnp.einsum(
        "ckgp,cpkd->ckgd", weights, values.astype(jnp.float32), precision=lax.Precision.HIGHEST
    )
    return (peak, total, summed)


def slot_plan(places_table, owner_table, length_table, anchor, step, count, capacity):
    seq_count, most_pages = places_table.shape
    entries = seq_count * most_pages
    positions = jnp.arange(entries, dtype=jnp.int32)
    sequence_lookup = positions // most_pages
    live = positions % most_pages < jnp.repeat(length_table, most_pages)
    page_starts = jnp.mod(owner_table.reshape(-1) - anchor, count)
    chosen = live & (page_starts == step)
    rank = jnp.cumsum(chosen.astype(jnp.int32)) - 1
    slot_numbers = jnp.arange(capacity, dtype=jnp.int32)
    picker = (chosen[None, :] & (rank[None, :] == slot_numbers[:, None])).astype(jnp.int32)
    used = jnp.sum(picker, axis=1)
    wanted = jnp.sum(picker * places_table.reshape(-1)[None, :], axis=1)
    seq_slot = jnp.sum(picker * sequence_lookup[None, :], axis=1)
    return (wanted, used, seq_slot)


def body(queries, new_kv, kv_pages, page_index, page_owner, seq_pages):
    count = lax.axis_size("store")
    myself = lax.axis_index("store")
    seq_count, most_pages = page_index.shape
    kv_count = new_kv.shape[2] // HEAD_DIM
    heads_per_group = queries.shape[1] // (kv_count * HEAD_DIM)
    entries = seq_count * most_pages
    capacity = entries // REACH
    scale = HEAD_DIM ** (-0.5)
    query_head_count = queries.reshape(seq_count, kv_count, heads_per_group, HEAD_DIM)
    peaks, totals, sums, slot_seqs, slot_used = ([], [], [], [], [])
    for step in range(REACH):
        wanted, used, seq_slot = slot_plan(
            page_index, page_owner, seq_pages, myself, step, count, capacity
        )
        query_rows = query_head_count[seq_slot]
        if step == 0:
            incoming = jnp.stack([wanted, used])
        else:
            incoming = shifted(jnp.stack([wanted, used]), "store", step)
        served = kv_pages[incoming[0]]
        if step == 0:
            partial_value = page_partial(query_rows, served, scale)
        else:
            foreign_shard_rows = shifted(query_rows, "store", step)
            partial_value = page_partial(foreign_shard_rows, served, scale)
            partial_value = shifted(
                (partial_value[0], partial_value[1], partial_value[2]), "store", -step
            )
        peaks.append(partial_value[0])
        totals.append(partial_value[1])
        sums.append(partial_value[2])
        slot_seqs.append(seq_slot)
        slot_used.append(used)
    peak = jnp.concatenate(peaks, axis=0)
    total = jnp.concatenate(totals, axis=0)
    summed = jnp.concatenate(sums, axis=0)
    member = (
        jnp.concatenate(slot_seqs)[None, :] == jnp.arange(seq_count, dtype=jnp.int32)[:, None]
    ) & (jnp.concatenate(slot_used)[None, :] > 0)
    fresh_key_rows = new_kv[:, 0].reshape(seq_count, kv_count, HEAD_DIM)
    new_values = new_kv[:, 1].reshape(seq_count, kv_count, HEAD_DIM).astype(jnp.float32)
    own = (
        jnp.einsum(
            "esnu,esu->esn", query_head_count, fresh_key_rows, preferred_element_type=jnp.float32
        )
        * scale
    )
    inside = member[:, :, None, None]
    highest = jnp.max(jnp.where(inside, peak[None], jnp.float32(-1e30)), axis=1)
    highest = jnp.maximum(highest, own)
    factor = jnp.where(
        inside, jnp.exp(jnp.where(inside, peak[None] - highest[:, None], 0.0)), jnp.float32(0.0)
    )
    own_weight = jnp.exp(own - highest)
    denominator = (
        jnp.einsum("bskg,skg->bkg", factor, total, precision=lax.Precision.HIGHEST) + own_weight
    )
    numerator = jnp.einsum("bskg,skgd->bkgd", factor, summed, precision=lax.Precision.HIGHEST)
    numerator = numerator + own_weight[..., None] * new_values[:, :, None, :]
    return (numerator / denominator[..., None]).reshape(seq_count, -1).astype(jnp.bfloat16)


def solution(mesh):
    in_specs = (
        P(("groups", "store"), "tensor"),
        P(("groups", "store"), None, "tensor"),
        P(("groups", "store"), None, None, "tensor"),
        P(("groups", "store"), None),
        P(("groups", "store"), None),
        P(("groups", "store")),
    )
    out_specs = P(("groups", "store"), "tensor")
    return jax.shard_map(body, mesh=mesh, in_specs=in_specs, out_specs=out_specs, check_vma=False)
```

profile of v0, /device:TPU:0, one launch (start us, length us, event | category | flops | bytes accessed | tf_op | source)
XLA Modules:
  0.0 62.0 jit_solution(17500604046748010121)
XLA Ops:
  0.0 0.7 %broadcast_subtract_fusion = s32[2,4]{1,0:T(2,128)S(1)} fusion(s32[2,4]{1,0:T(2,128)} %param.10, s32[]{:T(128)S(6)} %axis_index.15), kind=kLoop, calls=%fused_computation.126 | loop fusion | flops 8 | bytes 68 | tf_op jit(solution)/shard_map/sub | solution.py:39
  0.7 0.1 sub.142
  0.9 0.7 %broadcast_in_dim.23 = s32[2,4]{1,0:T(2,128)S(1)} broadcast(s32[2]{0:T(128)} %param.11), dimensions={0} | broadcast | bytes 40 | tf_op jit(solution)/shard_map/broadcast_in_dim | solution.py:38
  1.6 0.1 reshape.570
  1.7 0.8 %mul.93 = s32[8]{0:T(128)S(1)} reshape(s32[2,4]{1,0:T(2,128)} %param.9) | data formatting | bytes 64 | tf_op jit(solution)/shard_map/mul | solution.py:45
  2.5 0.2 reduce-window.35
  2.7 0.2 reduce-window.34
  2.9 0.2 reduce-window.33
  3.1 0.2 reduce-window.32
  3.3 0.3 convert_reduce_fusion
  3.6 4.0 %collective-permute-start.7 = (s32[2,2]{1,0:T(2,128)S(1)}, s32[2,2]{1,0:T(2,128)S(1)}, u32[]{:S(2)}, u32[]{:S(2)}) collective-permute-start(s32[2,2]{1,0:T(2,128)S(1)} %pad_add_fusion.2), channel_id=1, source_target_pairs={{0,6},{2,8},{4,10},{6,12},{8,14},{10,0},{12,2},{14,4},{1,7},{3,9},... | collective-permute-start | bytes 56 | tf_op jit(solution)/shard_map/ppermute | solution.py:13
  7.7 1.6 %collective-permute-start.4 = (s32[2,2]{1,0:T(2,128)S(1)}, s32[2,2]{1,0:T(2,128)S(1)}, u32[]{:S(2)}, u32[]{:S(2)}) collective-permute-start(s32[2,2]{1,0:T(2,128)S(1)} %pad_add_fusion.1), channel_id=1, source_target_pairs={{0,4},{2,6},{4,8},{6,10},{8,12},{10,14},{12,0},{14,2},{1,5},{3,7},... | collective-permute-start | bytes 56 | tf_op jit(solution)/shard_map/ppermute | solution.py:13
  9.2 1.5 %collective-permute-start.1 = (s32[2,2]{1,0:T(2,128)S(1)}, s32[2,2]{1,0:T(2,128)S(1)}, u32[]{:S(2)}, u32[]{:S(2)}) collective-permute-start(s32[2,2]{1,0:T(2,128)S(1)} %pad_add_fusion), channel_id=1, source_target_pairs={{0,2},{2,4},{4,6},{6,8},{8,10},{10,12},{12,14},{14,0},{1,3},{3,5},... | collective-permute-start | bytes 56 | tf_op jit(solution)/shard_map/ppermute | solution.py:13
  10.8 0.7 %copy.80 = bf16[1,2,32,128]{3,2,1,0:T(8,128)(2,1)S(1)} copy(bf16[1,2,32,128]{3,1,2,0:T(2,128)(2,1)} %bitcast.115) | data formatting | bytes 32768
  11.5 0.6 gather_fusion.2
  12.1 1.5 %collective-permute-start = (bf16[2,4,8,128]{3,2,1,0:T(8,128)(2,1)S(1)}, bf16[2,4,8,128]{3,2,1,0:T(8,128)(2,1)S(1)}, u32[]{:S(2)}, u32[]{:S(2)}) collective-permute-start(bf16[2,4,8,128]{3,2,1,0:T(8,128)(2,1)S(1)} %gather_fusion.2), channel_id=1, source_target_pairs={{0,2},{2,4},{4,6},{6,8},{8,10},{10,12},{12,14},{14,0},{1,3},{3,5},... | collective-permute-start | bytes 49160 | tf_op jit(solution)/shard_map/ppermute | solution.py:13
  13.6 0.6 gather_fusion.4
  14.2 0.3 collective-permute-start.3
  14.5 0.7 %slice_convert_fusion = f32[2,1,512]{2,1,0:T(1,128)S(1)} fusion(bf16[2,2,512]{2,1,0:T(2,128)(2,1)} %param.7), kind=kLoop, calls=%fused_computation.59 | loop fusion | flops 1024 | bytes 6144 | tf_op jit(solution)/shard_map/convert_element_type | solution.py:91
  15.2 0.8 %fusion.24 = f32[2,4,1,8]{3,2,1,0:T(1,128)S(1)} fusion(bf16[2,4,8,128]{3,2,1,0:T(8,128)(2,1)S(1)} %bitcast.111, bf16[2,2,512]{2,1,0:T(2,128)(2,1)} %param.7), kind=kOutput, calls=%fused_computation.57 | convolution fusion | flops 16384 | bytes 20736 | tf_op jit(solution)/shard_map/esnu,esu->esn/dot_general | solution.py:93
  16.2 0.1 copy.73
  16.3 0.6 gather_fusion.6
  16.8 0.6 gather_fusion
  17.4 2.8 %gather_fusion.1 = bf16[2,2,256,512]{3,2,1,0:T(8,128)(2,1)S(1)} fusion(bf16[8,2,256,512]{3,2,1,0:T(8,128)(2,1)} %param.8, s32[1024]{0:T(1024)S(1)} %pad_clamp_fusion.6), kind=kCustom, calls=%fused_computation.1 | custom fusion | bytes 2097160 | tf_op jit(solution)/shard_map/gather | solution.py:70
  20.3 0.2 copy.45
  20.5 0.2 copy.47
  20.7 0.3 fusion.51
  21.0 0.2 fusion.4
  21.1 0.6 fusion.5
  21.7 2.6 %collective-permute-start.6 = (bf16[2,4,8,128]{3,2,1,0:T(8,128)(2,1)S(1)}, bf16[2,4,8,128]{3,2,1,0:T(8,128)(2,1)S(1)}, u32[]{:S(2)}, u32[]{:S(2)}) collective-permute-start(bf16[2,4,8,128]{3,2,1,0:T(8,128)(2,1)S(1)} %gather_fusion.6), channel_id=1, source_target_pairs={{0,6},{2,8},{4,10},{6,12},{8,14},{10,0},{12,2},{14,4},{1,7},{3,9},... | collective-permute-start | bytes 49160 | tf_op jit(solution)/shard_map/ppermute | solution.py:13
  24.4 2.8 %gather_fusion.3 = bf16[2,2,256,512]{3,2,1,0:T(8,128)(2,1)S(1)} fusion(bf16[8,2,256,512]{3,2,1,0:T(8,128)(2,1)} %param.8, s32[1024]{0:T(1024)S(1)} %pad_clamp_fusion.4), kind=kCustom, calls=%fused_computation.3 | custom fusion | bytes 2097160 | tf_op jit(solution)/shard_map/gather | solution.py:70
  27.3 2.8 %gather_fusion.5 = bf16[2,2,256,512]{3,2,1,0:T(8,128)(2,1)S(1)} fusion(bf16[8,2,256,512]{3,2,1,0:T(8,128)(2,1)} %param.8, s32[1024]{0:T(1024)S(1)} %pad_clamp_fusion.2), kind=kCustom, calls=%fused_computation.5 | custom fusion | bytes 2097160 | tf_op jit(solution)/shard_map/gather | solution.py:70
  30.1 1.1 %fusion.46 = (bf16[2,1,256,512]{3,2,1,0:T(8,128)(2,1)}, bf16[2,1,256,512]{3,2,1,0:T(8,128)(2,1)}) fusion(bf16[2,2,256,512]{3,2,1,0:T(8,128)(2,1)S(1)} %gather_fusion.5), kind=kLoop, calls=%fused_computation.133 | loop fusion | bytes 2097152 | tf_op jit(solution)/shard_map/slice | solution.py:19
  31.2 2.8 %gather_fusion.7 = bf16[2,2,256,512]{3,2,1,0:T(8,128)(2,1)S(1)} fusion(bf16[8,2,256,512]{3,2,1,0:T(8,128)(2,1)} %param.8, s32[1024]{0:T(1024)S(1)} %pad_clamp_fusion), kind=kCustom, calls=%fused_computation.7 | custom fusion | bytes 2097160 | tf_op jit(solution)/shard_map/gather | solution.py:70
  34.0 1.1 %fusion.47 = (bf16[2,1,256,512]{3,2,1,0:T(8,128)(2,1)}, bf16[2,1,256,512]{3,2,1,0:T(8,128)(2,1)}) fusion(bf16[2,2,256,512]{3,2,1,0:T(8,128)(2,1)S(1)} %gather_fusion.7), kind=kLoop, calls=%fused_computation.134 | loop fusion | bytes 2097152 | tf_op jit(solution)/shard_map/slice | solution.py:19
  35.1 0.2 copy.49
  35.3 0.2 copy.51
  35.5 1.2 %copy.53 = bf16[2,1,256,512]{2,3,0,1:T(8,128)(2,1)S(1)} copy(bf16[2,1,256,512]{3,2,1,0:T(8,128)(2,1)} %get-tuple-element.29) | data formatting | bytes 1048576 | tf_op jit(solution)/shard_map/slice | solution.py:19
  36.8 1.2 %copy.55 = bf16[2,1,256,512]{2,3,0,1:T(8,128)(2,1)S(1)} copy(bf16[2,1,256,512]{3,2,1,0:T(8,128)(2,1)} %get-tuple-element.30) | data formatting | bytes 1048576 | tf_op jit(solution)/shard_map/slice | solution.py:20
  38.0 1.2 %copy.57 = bf16[2,1,256,512]{2,3,0,1:T(8,128)(2,1)S(1)} copy(bf16[2,1,256,512]{3,2,1,0:T(8,128)(2,1)} %get-tuple-element.31) | data formatting | bytes 1048576 | tf_op jit(solution)/shard_map/slice | solution.py:19
  39.3 1.2 %copy.59 = bf16[2,1,256,512]{2,3,0,1:T(8,128)(2,1)S(1)} copy(bf16[2,1,256,512]{3,2,1,0:T(8,128)(2,1)} %get-tuple-element.32) | data formatting | bytes 1048576 | tf_op jit(solution)/shard_map/slice | solution.py:20
  40.5 0.3 fusion.50
  40.8 2.3 %collective-permute-start.9 = (f32[2,4,8]{2,1,0:T(4,128)S(1)}, f32[2,4,8]{2,1,0:T(4,128)S(1)}, u32[]{:S(2)}, u32[]{:S(2)}) collective-permute-start(f32[2,4,8]{2,1,0:T(4,128)S(1)} %get-tuple-element.43), channel_id=1, source_target_pairs={{0,14},{2,0},{4,2},{6,4},{8,6},{10,8},{12,10},{14,12},{1,15},{3,1}... | collective-permute-start | bytes 776 | tf_op jit(solution)/shard_map/ppermute | solution.py:13
  43.1 0.2 fusion.6
  43.3 0.6 collective-permute-start.12
  43.8 0.6 fusion.7
  44.4 0.3 fusion.49
  44.7 1.2 %collective-permute-start.10 = (f32[2,4,8]{2,1,0:T(4,128)S(1)}, f32[2,4,8]{2,1,0:T(4,128)S(1)}, u32[]{:S(2)}, u32[]{:S(2)}) collective-permute-start(f32[2,4,8]{2,1,0:T(4,128)S(1)} %get-tuple-element.41), channel_id=1, source_target_pairs={{0,12},{2,14},{4,0},{6,2},{8,4},{10,6},{12,8},{14,10},{1,13},{3,15... | collective-permute-start | bytes 776 | tf_op jit(solution)/shard_map/ppermute | solution.py:13
  45.9 0.2 fusion.8
  46.1 2.0 %collective-permute-start.13 = (f32[2,4,8]{2,1,0:T(4,128)S(1)}, f32[2,4,8]{2,1,0:T(4,128)S(1)}, u32[]{:S(2)}, u32[]{:S(2)}) collective-permute-start(f32[2,4,8]{2,1,0:T(4,128)S(1)} %fusion.8), channel_id=1, source_target_pairs={{0,12},{2,14},{4,0},{6,2},{8,4},{10,6},{12,8},{14,10},{1,13},{3,15... | collective-permute-start | bytes 776 | tf_op jit(solution)/shard_map/ppermute | solution.py:13
  48.1 0.6 fusion.9
  48.6 0.3 fusion.48
  48.9 0.2 fusion.10
  49.1 1.3 %collective-permute-start.14 = (f32[2,4,8]{2,1,0:T(4,128)S(1)}, f32[2,4,8]{2,1,0:T(4,128)S(1)}, u32[]{:S(2)}, u32[]{:S(2)}) collective-permute-start(f32[2,4,8]{2,1,0:T(4,128)S(1)} %fusion.10), channel_id=1, source_target_pairs={{0,10},{2,12},{4,14},{6,0},{8,2},{10,4},{12,6},{14,8},{1,11},{3,13... | collective-permute-start | bytes 776 | tf_op jit(solution)/shard_map/ppermute | solution.py:13
  50.4 0.6 fusion.11
  51.0 1.2 %collective-permute-start.11 = (f32[2,4,8]{2,1,0:T(4,128)S(1)}, f32[2,4,8]{2,1,0:T(4,128)S(1)}, u32[]{:S(2)}, u32[]{:S(2)}) collective-permute-start(f32[2,4,8]{2,1,0:T(4,128)S(1)} %get-tuple-element.39), channel_id=1, source_target_pairs={{0,10},{2,12},{4,14},{6,0},{8,2},{10,4},{12,6},{14,8},{1,11},{3,13... | collective-permute-start | bytes 776 | tf_op jit(solution)/shard_map/ppermute | solution.py:13
  52.2 3.8 %collective-permute-start.2 = (f32[2,4,8,128]{3,2,1,0:T(8,128)S(1)}, f32[2,4,8,128]{3,2,1,0:T(8,128)S(1)}, u32[]{:S(2)}, u32[]{:S(2)}) collective-permute-start(f32[2,4,8,128]{3,2,1,0:T(8,128)S(1)} %fusion.7), channel_id=1, source_target_pairs={{0,14},{2,0},{4,2},{6,4},{8,6},{10,8},{12,10},{14,12},{1,15},{3,1}... | collective-permute-start | bytes 98312 | tf_op jit(solution)/shard_map/ppermute | solution.py:13
  56.1 0.3 collective-permute-start.8
  56.5 0.1 select_reduce_fusion
  56.6 0.4 fusion.16
  57.0 0.5 collective-permute-done.2
  57.6 2.3 %collective-permute-done.5 = f32[2,4,8,128]{3,2,1,0:T(8,128)S(1)} collective-permute-done((f32[2,4,8,128]{3,2,1,0:T(8,128)S(1)}, f32[2,4,8,128]{3,2,1,0:T(8,128)S(1)}, u32[]{:S(2)}, u32[]{:S(2)}) %collective-permute-start.5) | collective-permute-done | bytes 32800 | tf_op jit(solution)/shard_map/ppermute | solution.py:13
  59.9 1.0 %collective-permute-done.8 = f32[2,4,8,128]{3,2,1,0:T(8,128)S(1)} collective-permute-done((f32[2,4,8,128]{3,2,1,0:T(8,128)S(1)}, f32[2,4,8,128]{3,2,1,0:T(8,128)S(1)}, u32[]{:S(2)}, u32[]{:S(2)}) %collective-permute-start.8) | collective-permute-done | bytes 32800 | tf_op jit(solution)/shard_map/ppermute | solution.py:13
  60.9 1.1 %fusion.2 = bf16[2,4,8,128]{3,0,2,1:T(2,128)(2,1)} fusion(f32[8,4,8,128]{3,2,1,0:T(8,128)S(1)} %pad_maximum_fusion, pred[2,8]{1,0:T(4,128)(4,1)S(1)} %compare_and_fusion, f32[2,4,8]{0,2,1:T(8,128)S(1)} %get-tuple-element.17, f32[2,4,128]{2,0,1:T(2,128)S(1)} %copy.63, f32[2,4,8]{0,2,1:T(8,128)S(1)} %get-tuple-element.18, f32[2,4,8]{0,2,1:T(8,128)S(1)} %fusion.23, ...), kind=kOutput, calls=%fused_computation.15 | convolution fusion | flops 820736 | bytes 153360 | tf_op jit(solution)/shard_map/bskg,skgd->bkgd/dot_general | solution.py:108
  (54 shorter events, 0.9 us)
Async XLA Ops:
  3.6 18.1 %collective-permute-start.7 = (s32[2,2]{1,0:T(2,128)S(1)}, s32[2,2]{1,0:T(2,128)S(1)}, u32[]{:S(2)}, u32[]{:S(2)}) collective-permute-start(s32[2,2]{1,0:T(2,128)S(1)} %pad_add_fusion.2), channel_id=1, source_target_pairs={{0,6},{2,8},{4,10},{6,12},{8,14},{10,0},{12,2},{14,4},{1,7},{3,9},... | collective-permute-start | bytes 56 | tf_op jit(solution)/shard_map/ppermute | solution.py:13
  7.7 16.7 %collective-permute-start.4 = (s32[2,2]{1,0:T(2,128)S(1)}, s32[2,2]{1,0:T(2,128)S(1)}, u32[]{:S(2)}, u32[]{:S(2)}) collective-permute-start(s32[2,2]{1,0:T(2,128)S(1)} %pad_add_fusion.1), channel_id=1, source_target_pairs={{0,4},{2,6},{4,8},{6,10},{8,12},{10,14},{12,0},{14,2},{1,5},{3,7},... | collective-permute-start | bytes 56 | tf_op jit(solution)/shard_map/ppermute | solution.py:13
  9.2 15.2 %collective-permute-start.1 = (s32[2,2]{1,0:T(2,128)S(1)}, s32[2,2]{1,0:T(2,128)S(1)}, u32[]{:S(2)}, u32[]{:S(2)}) collective-permute-start(s32[2,2]{1,0:T(2,128)S(1)} %pad_add_fusion), channel_id=1, source_target_pairs={{0,2},{2,4},{4,6},{6,8},{8,10},{10,12},{12,14},{14,0},{1,3},{3,5},... | collective-permute-start | bytes 56 | tf_op jit(solution)/shard_map/ppermute | solution.py:13
  12.1 28.4 %collective-permute-start = (bf16[2,4,8,128]{3,2,1,0:T(8,128)(2,1)S(1)}, bf16[2,4,8,128]{3,2,1,0:T(8,128)(2,1)S(1)}, u32[]{:S(2)}, u32[]{:S(2)}) collective-permute-start(bf16[2,4,8,128]{3,2,1,0:T(8,128)(2,1)S(1)} %gather_fusion.2), channel_id=1, source_target_pairs={{0,2},{2,4},{4,6},{6,8},{8,10},{10,12},{12,14},{14,0},{1,3},{3,5},... | collective-permute-start | bytes 49160 | tf_op jit(solution)/shard_map/ppermute | solution.py:13
  14.2 30.2 %collective-permute-start.3 = (bf16[2,4,8,128]{3,2,1,0:T(8,128)(2,1)S(1)}, bf16[2,4,8,128]{3,2,1,0:T(8,128)(2,1)S(1)}, u32[]{:S(2)}, u32[]{:S(2)}) collective-permute-start(bf16[2,4,8,128]{3,2,1,0:T(8,128)(2,1)S(1)} %gather_fusion.4), channel_id=1, source_target_pairs={{0,4},{2,6},{4,8},{6,10},{8,12},{10,14},{12,0},{14,2},{1,5},{3,7},... | collective-permute-start | bytes 49160 | tf_op jit(solution)/shard_map/ppermute | solution.py:13
  21.7 26.9 %collective-permute-start.6 = (bf16[2,4,8,128]{3,2,1,0:T(8,128)(2,1)S(1)}, bf16[2,4,8,128]{3,2,1,0:T(8,128)(2,1)S(1)}, u32[]{:S(2)}, u32[]{:S(2)}) collective-permute-start(bf16[2,4,8,128]{3,2,1,0:T(8,128)(2,1)S(1)} %gather_fusion.6), channel_id=1, source_target_pairs={{0,6},{2,8},{4,10},{6,12},{8,14},{10,0},{12,2},{14,4},{1,7},{3,9},... | collective-permute-start | bytes 49160 | tf_op jit(solution)/shard_map/ppermute | solution.py:13
  40.8 15.3 %collective-permute-start.9 = (f32[2,4,8]{2,1,0:T(4,128)S(1)}, f32[2,4,8]{2,1,0:T(4,128)S(1)}, u32[]{:S(2)}, u32[]{:S(2)}) collective-permute-start(f32[2,4,8]{2,1,0:T(4,128)S(1)} %get-tuple-element.43), channel_id=1, source_target_pairs={{0,14},{2,0},{4,2},{6,4},{8,6},{10,8},{12,10},{14,12},{1,15},{3,1}... | collective-permute-start | bytes 776 | tf_op jit(solution)/shard_map/ppermute | solution.py:13
  43.3 7.7 %collective-permute-start.12 = (f32[2,4,8]{2,1,0:T(4,128)S(1)}, f32[2,4,8]{2,1,0:T(4,128)S(1)}, u32[]{:S(2)}, u32[]{:S(2)}) collective-permute-start(f32[2,4,8]{2,1,0:T(4,128)S(1)} %fusion.6), channel_id=1, source_target_pairs={{0,14},{2,0},{4,2},{6,4},{8,6},{10,8},{12,10},{14,12},{1,15},{3,1}... | collective-permute-start | bytes 776 | tf_op jit(solution)/shard_map/ppermute | solution.py:13
  44.7 11.7 %collective-permute-start.10 = (f32[2,4,8]{2,1,0:T(4,128)S(1)}, f32[2,4,8]{2,1,0:T(4,128)S(1)}, u32[]{:S(2)}, u32[]{:S(2)}) collective-permute-start(f32[2,4,8]{2,1,0:T(4,128)S(1)} %get-tuple-element.41), channel_id=1, source_target_pairs={{0,12},{2,14},{4,0},{6,2},{8,4},{10,6},{12,8},{14,10},{1,13},{3,15... | collective-permute-start | bytes 776 | tf_op jit(solution)/shard_map/ppermute | solution.py:13
  46.1 6.1 %collective-permute-start.13 = (f32[2,4,8]{2,1,0:T(4,128)S(1)}, f32[2,4,8]{2,1,0:T(4,128)S(1)}, u32[]{:S(2)}, u32[]{:S(2)}) collective-permute-start(f32[2,4,8]{2,1,0:T(4,128)S(1)} %fusion.8), channel_id=1, source_target_pairs={{0,12},{2,14},{4,0},{6,2},{8,4},{10,6},{12,8},{14,10},{1,13},{3,15... | collective-permute-start | bytes 776 | tf_op jit(solution)/shard_map/ppermute | solution.py:13
  49.1 6.9 %collective-permute-start.14 = (f32[2,4,8]{2,1,0:T(4,128)S(1)}, f32[2,4,8]{2,1,0:T(4,128)S(1)}, u32[]{:S(2)}, u32[]{:S(2)}) collective-permute-start(f32[2,4,8]{2,1,0:T(4,128)S(1)} %fusion.10), channel_id=1, source_target_pairs={{0,10},{2,12},{4,14},{6,0},{8,2},{10,4},{12,6},{14,8},{1,11},{3,13... | collective-permute-start | bytes 776 | tf_op jit(solution)/shard_map/ppermute | solution.py:13
  51.0 5.4 %collective-permute-start.11 = (f32[2,4,8]{2,1,0:T(4,128)S(1)}, f32[2,4,8]{2,1,0:T(4,128)S(1)}, u32[]{:S(2)}, u32[]{:S(2)}) collective-permute-start(f32[2,4,8]{2,1,0:T(4,128)S(1)} %get-tuple-element.39), channel_id=1, source_target_pairs={{0,10},{2,12},{4,14},{6,0},{8,2},{10,4},{12,6},{14,8},{1,11},{3,13... | collective-permute-start | bytes 776 | tf_op jit(solution)/shard_map/ppermute | solution.py:13
  52.2 5.4 %collective-permute-start.2 = (f32[2,4,8,128]{3,2,1,0:T(8,128)S(1)}, f32[2,4,8,128]{3,2,1,0:T(8,128)S(1)}, u32[]{:S(2)}, u32[]{:S(2)}) collective-permute-start(f32[2,4,8,128]{3,2,1,0:T(8,128)S(1)} %fusion.7), channel_id=1, source_target_pairs={{0,14},{2,0},{4,2},{6,4},{8,6},{10,8},{12,10},{14,12},{1,15},{3,1}... | collective-permute-start | bytes 98312 | tf_op jit(solution)/shard_map/ppermute | solution.py:13
  56.0 3.9 %collective-permute-start.5 = (f32[2,4,8,128]{3,2,1,0:T(8,128)S(1)}, f32[2,4,8,128]{3,2,1,0:T(8,128)S(1)}, u32[]{:S(2)}, u32[]{:S(2)}) collective-permute-start(f32[2,4,8,128]{3,2,1,0:T(8,128)S(1)} %fusion.9), channel_id=1, source_target_pairs={{0,12},{2,14},{4,0},{6,2},{8,4},{10,6},{12,8},{14,10},{1,13},{3,15... | collective-permute-start | bytes 98312 | tf_op jit(solution)/shard_map/ppermute | solution.py:13
  56.1 4.8 %collective-permute-start.8 = (f32[2,4,8,128]{3,2,1,0:T(8,128)S(1)}, f32[2,4,8,128]{3,2,1,0:T(8,128)S(1)}, u32[]{:S(2)}, u32[]{:S(2)}) collective-permute-start(f32[2,4,8,128]{3,2,1,0:T(8,128)S(1)} %fusion.11), channel_id=1, source_target_pairs={{0,10},{2,12},{4,14},{6,0},{8,2},{10,4},{12,6},{14,8},{1,11},{3,13... | collective-permute-start | bytes 98312 | tf_op jit(solution)/shard_map/ppermute | solution.py:13
where the time goes:
time: 62.6 us; the launch traced here: 62 us
  local copies, waits for them, and re-layouts  24.3 us (39%)
  starting transfers between devices  24.3 us (39%)
  matrix products  5.57 us (9%)
  waiting for transfers between devices  3.87 us (6%)
  other arithmetic  3.58 us (6%)
    ppermute x15, starting transfers between devices, shifted(): return lax.ppermute(value, axis, pairs)  24.3 us
    gather x4, local copies, waits for them, and re-layouts, body(): served = kv_pages[incoming[0]]  11.2 us
    slice x8, local copies, waits for them, and re-layouts, page_partial(): keys = served[:, 0].reshape(slots, length, kv_count, width // kv_count)  5.2 us
    ppermute x15, waiting for transfers between devices, shifted(): return lax.ppermute(value, axis, pairs)  3.87 us
    slice x4, local copies, waits for them, and re-layouts, page_partial(): values = served[:, 1].reshape(slots, length, kv_count, width // kv_count)  2.9 us
    gather x4, local copies, waits for them, and re-layouts, body(): query_rows = query_head_count[seq_slot]  2.23 us
    dot_general x4, matrix products, page_partial(): jnp.einsum('ckgp,cpkd->ckgd', weights, values.astype(jnp.float32), precis...  2.22 us
  transfers between devices with their start and end apart: 15, of which 3 were waited for; matrix products, arithmetic and copies ran while one was open for 46% of the time, Pallas kernels for 0%

commit v1 on v0

v1 whole, which is shorter than its diff:
```python
import functools

import jax
import jax.numpy as jnp
from jax import lax
from jax.experimental import pallas as pl
from jax.experimental.pallas import tpu as pltpu
from jax.sharding import PartitionSpec as P

HEAD_DIM = 128
REACH = 4
TILE = 8
PACKED_TILE = 16
NEVER = -1e30
VMEM = pl.BlockSpec(memory_space=pltpu.VMEM)
PARAMS = pltpu.CompilerParams(vmem_limit_bytes=16 * 2**20)
SMEM = pl.BlockSpec(memory_space=pltpu.SMEM)


def shifted(value, axis, steps):
    count = lax.axis_size(axis)
    pairs = [(source, (source + steps) % count) for source in range(count)]
    return lax.ppermute(value, axis, pairs)


def slot_plan(owner_ref, length_ref, places_ref, count, capacity):
    myself = lax.axis_index("store")
    seq_count, most_pages = owner_ref.shape
    zero = jnp.int32(0)
    plan = [[(zero, zero, zero) for _ in range(capacity)] for _ in range(REACH)]
    taken = [zero for _ in range(REACH)]
    for seq in range(seq_count):
        for page in range(most_pages):
            live = page < length_ref[seq]
            gap = owner_ref[seq, page] - myself
            gap = jnp.where(gap < 0, gap + count, gap)
            place = places_ref[seq, page] if places_ref is not None else zero
            for step in range(REACH):
                mine = live & (gap == step)
                for slot in range(capacity):
                    here = mine & (taken[step] == slot)
                    old = plan[step][slot]
                    plan[step][slot] = (
                        jnp.where(here, jnp.int32(seq), old[0]),
                        jnp.where(here, place, old[1]),
                        jnp.where(here, jnp.int32(1), old[2]),
                    )
                taken[step] = taken[step] + mine.astype(jnp.int32)
    return plan


def first_kernel(out_ref):
    out_ref[...] = jnp.zeros_like(out_ref)


def pack_kernel(count, capacity, first_ref, owner_ref, length_ref, places_ref, queries_ref, *refs):
    outs, rows = refs[:-1], refs[-1]
    seq_count = queries_ref.shape[0]
    heads = queries_ref.shape[1] // HEAD_DIM
    for head in range(heads):
        rows[pl.ds(head, seq_count, stride=heads), :] = queries_ref[
            :, head * HEAD_DIM : (head + 1) * HEAD_DIM
        ].astype(jnp.float32)
    plan = slot_plan(owner_ref, length_ref, places_ref, count, capacity)
    line = lax.broadcasted_iota(jnp.int32, (PACKED_TILE, HEAD_DIM), 0)
    for step in range(REACH):
        note = jnp.zeros((PACKED_TILE, HEAD_DIM), jnp.int32)
        for slot in range(capacity):
            seq, place, _ = plan[step][slot]
            value = rows[0:heads, :]
            for other in range(1, seq_count):
                value = jnp.where(seq == other, rows[other * heads : (other + 1) * heads, :], value)
            outs[step][slot * heads : (slot + 1) * heads, :] = value.astype(jnp.bfloat16)
            note = jnp.where(line == slot, place, note)
        outs[step][capacity * heads :, :] = note.astype(jnp.float32).astype(jnp.bfloat16)


def page_parts(payload_ref, pages_ref, slot, heads, capacity, scale):
    kv_count = pages_ref.shape[3] // HEAD_DIM
    group = heads // kv_count
    notes = payload_ref[capacity * heads :, :].astype(jnp.float32)
    place = notes[slot, 0].astype(jnp.int32)
    query = payload_ref[slot * heads : (slot + 1) * heads, :].astype(jnp.float32)
    row_group = lax.broadcasted_iota(jnp.int32, query.shape, 0) // group
    spread = jnp.concatenate(
        [jnp.where(row_group == kv, query, 0.0) for kv in range(kv_count)], axis=1
    ).astype(jnp.bfloat16)
    scores = lax.dot_general(
        spread, pages_ref[place, 0], (((1,), (1,)), ((), ())), preferred_element_type=jnp.float32
    ) * scale
    peak = jnp.max(scores, axis=1, keepdims=True)
    weights = jnp.exp(scores - peak)
    total = jnp.sum(weights, axis=1, keepdims=True)
    high = weights.astype(jnp.bfloat16)
    low = (weights - high.astype(jnp.float32)).astype(jnp.bfloat16)
    both = jnp.dot(
        jnp.concatenate([high, low], axis=0), pages_ref[place, 1], preferred_element_type=jnp.float32
    )
    wide = both[:heads] + both[heads:]
    summed = [
        wide[kv * group : (kv + 1) * group, kv * HEAD_DIM : (kv + 1) * HEAD_DIM]
        for kv in range(kv_count)
    ]
    return peak, total, jnp.concatenate(summed, axis=0)


def to_lanes(column, offset):
    shape = (column.shape[0], HEAD_DIM)
    at = lax.broadcasted_iota(jnp.int32, shape, 0) + offset
    lane = lax.broadcasted_iota(jnp.int32, shape, 1)
    return jnp.sum(jnp.where(at == lane, column, 0.0), axis=0, keepdims=True)


def to_column(row, offset, heads):
    shape = (heads, HEAD_DIM)
    at = lax.broadcasted_iota(jnp.int32, shape, 0) + offset
    lane = lax.broadcasted_iota(jnp.int32, shape, 1)
    return jnp.sum(jnp.where(at == lane, row, 0.0), axis=1, keepdims=True)


def attend_kernel(heads, capacity, scale, payload_ref, pages_ref, out_ref):
    row = jnp.zeros((1, HEAD_DIM), jnp.float32)
    for slot in range(capacity):
        peak, total, summed = page_parts(payload_ref, pages_ref, slot, heads, capacity, scale)
        out_ref[slot * heads : (slot + 1) * heads, :] = summed
        row = row + to_lanes(peak, slot * heads) + to_lanes(total, (capacity + slot) * heads)
    out_ref[capacity * heads :, :] = jnp.broadcast_to(row, (TILE, HEAD_DIM))


def local_kernel(
    count, capacity, scale, owner_ref, length_ref, queries_ref, fresh_ref, payload_ref, pages_ref,
    state_ref, bias_ref, rows
):
    seq_count = queries_ref.shape[0]
    heads = queries_ref.shape[1] // HEAD_DIM
    kv_count = fresh_ref.shape[2] // HEAD_DIM
    group = heads // kv_count
    plan = slot_plan(owner_ref, length_ref, None, count, capacity)
    for head in range(heads):
        rows[pl.ds(head, seq_count, stride=heads), :] = queries_ref[
            :, head * HEAD_DIM : (head + 1) * HEAD_DIM
        ].astype(jnp.float32)
    slots = [
        (plan[0][slot][0], plan[0][slot][2])
        + page_parts(payload_ref, pages_ref, slot, heads, capacity, scale)
        for slot in range(capacity)
    ]
    row = jnp.zeros((1, HEAD_DIM), jnp.float32)
    for seq in range(seq_count):
        query = rows[seq * heads : (seq + 1) * heads, :]

        def fresh(which):
            line = fresh_ref[seq, which : which + 1, :].astype(jnp.float32)
            return jnp.concatenate(
                [
                    jnp.broadcast_to(line[:, kv * HEAD_DIM : (kv + 1) * HEAD_DIM], (group, HEAD_DIM))
                    for kv in range(kv_count)
                ],
                axis=0,
            )

        own = jnp.sum(query * fresh(0), axis=1, keepdims=True) * scale
        highest = own
        for at, used, peak, _, _ in slots:
            inside = (used > 0) & (at == seq)
            highest = jnp.maximum(highest, jnp.where(inside, peak, NEVER))
        own_weight = jnp.exp(own - highest)
        denominator = own_weight
        numerator = own_weight * fresh(1)
        for at, used, peak, total, summed in slots:
            inside = (used > 0) & (at == seq)
            factor = jnp.exp(jnp.where(inside, peak - highest, NEVER))
            denominator = denominator + factor * total
            numerator = numerator + factor * summed
        state_ref[seq * heads : (seq + 1) * heads, :] = numerator
        row = row + to_lanes(highest, seq * heads) + to_lanes(denominator, (seq_count + seq) * heads)
    state_ref[seq_count * heads :, :] = jnp.broadcast_to(row, (TILE, HEAD_DIM))
    line = lax.broadcasted_iota(jnp.int32, (TILE, HEAD_DIM), 0)
    lane = lax.broadcasted_iota(jnp.int32, (TILE, HEAD_DIM), 1)
    for step in range(1, REACH):
        bias = jnp.full((TILE, HEAD_DIM), NEVER, jnp.float32)
        for slot in range(capacity):
            at, _, used = plan[step][slot]
            mine = (line == at) & (lane // heads == slot) & (used > 0)
            bias = jnp.where(mine, 0.0, bias)
        bias_ref[(step - 1) * TILE : step * TILE, :] = bias


def combine_kernel(seq_count, capacity, state_ref, bias_ref, *refs):
    parts, out_ref, rows = refs[:-2], refs[-2], refs[-1]
    heads = out_ref.shape[1] // HEAD_DIM
    state_row = state_ref[seq_count * heads : seq_count * heads + 1, :]
    for seq in range(seq_count):
        base = to_column(state_row, seq * heads, heads)
        highest = base
        slots = []
        for step, part in enumerate(parts):
            row = part[capacity * heads : capacity * heads + 1, :]
            masked = row + bias_ref[step * TILE + seq : step * TILE + seq + 1, :]
            for slot in range(capacity):
                peak = to_column(masked, slot * heads, heads)
                total = to_column(row, (capacity + slot) * heads, heads)
                slots.append((peak, total, part[slot * heads : (slot + 1) * heads, :]))
                highest = jnp.maximum(highest, peak)
        factor = jnp.exp(base - highest)
        denominator = factor * to_column(state_row, (seq_count + seq) * heads, heads)
        numerator = factor * state_ref[seq * heads : (seq + 1) * heads, :]
        for peak, total, summed in slots:
            factor = jnp.exp(peak - highest)
            denominator = denominator + factor * total
            numerator = numerator + factor * summed
        rows[seq * heads : (seq + 1) * heads, :] = numerator / denominator
    for head in range(heads):
        out_ref[:, head * HEAD_DIM : (head + 1) * HEAD_DIM] = rows[
            pl.ds(head, seq_count, stride=heads), :
        ].astype(jnp.bfloat16)


def body(queries, new_kv, kv_pages, page_index, page_owner, seq_pages):
    count = lax.axis_size("store")
    seq_count, most_pages = page_index.shape
    capacity = seq_count * most_pages // REACH
    heads = queries.shape[1] // HEAD_DIM
    scale = HEAD_DIM ** (-0.5)
    slot_rows = capacity * heads
    assert kv_pages.shape[0] <= 256 and 2 * slot_rows <= HEAD_DIM and seq_count <= TILE
    sent = jax.ShapeDtypeStruct((slot_rows + PACKED_TILE, HEAD_DIM), jnp.bfloat16)
    back = jax.ShapeDtypeStruct((slot_rows + TILE, HEAD_DIM), jnp.float32)
    scratch = [pltpu.VMEM((seq_count * heads, HEAD_DIM), jnp.float32)]
    first = pl.pallas_call(
        first_kernel,
        out_shape=jax.ShapeDtypeStruct((TILE, HEAD_DIM), jnp.float32),
        out_specs=VMEM,
        compiler_params=PARAMS,
        cost_estimate=pl.CostEstimate(flops=2*10**9, bytes_accessed=0, transcendentals=0),
        name="first",
    )()
    payloads = pl.pallas_call(
        functools.partial(pack_kernel, count, capacity),
        out_shape=[sent] * REACH,
        in_specs=[VMEM] + [SMEM] * 3 + [VMEM],
        out_specs=[VMEM] * REACH,
        scratch_shapes=scratch,
        compiler_params=PARAMS,
        name="pack",
        cost_estimate=pl.CostEstimate(flops=10**12, bytes_accessed=0, transcendentals=0),
    )(first, page_owner, seq_pages, page_index, queries)
    attend = pl.pallas_call(
        functools.partial(attend_kernel, heads, capacity, scale),
        out_shape=back,
        in_specs=[VMEM] * 2,
        out_specs=VMEM,
        compiler_params=PARAMS,
        name="attend",
    )
    pages = kv_pages
    parts = [
        shifted(attend(shifted(payloads[step], "store", step), pages), "store", -step)
        for step in range(1, REACH)
    ]
    state, bias = pl.pallas_call(
        functools.partial(local_kernel, count, capacity, scale),
        out_shape=[
            jax.ShapeDtypeStruct((seq_count * heads + TILE, HEAD_DIM), jnp.float32),
            jax.ShapeDtypeStruct(((REACH - 1) * TILE, HEAD_DIM), jnp.float32),
        ],
        in_specs=[SMEM] * 2 + [VMEM] * 4,
        out_specs=[VMEM] * 2,
        scratch_shapes=scratch,
        compiler_params=PARAMS,
        name="local",
    )(page_owner, seq_pages, queries, new_kv, payloads[0], pages)
    return pl.pallas_call(
        functools.partial(combine_kernel, seq_count, capacity),
        out_shape=jax.ShapeDtypeStruct(queries.shape, queries.dtype),
        in_specs=[VMEM] * (1 + REACH),
        out_specs=VMEM,
        scratch_shapes=scratch,
        compiler_params=PARAMS,
        name="combine",
    )(state, bias, *parts)


def solution(mesh):
    in_specs = (
        P(("groups", "store"), "tensor"),
        P(("groups", "store"), None, "tensor"),
        P(("groups", "store"), None, None, "tensor"),
        P(("groups", "store"), None),
        P(("groups", "store"), None),
        P(("groups", "store")),
    )
    out_specs = P(("groups", "store"), "tensor")
    return jax.shard_map(body, mesh=mesh, in_specs=in_specs, out_specs=out_specs, check_vma=False)
```

time: 62.6 us -> 20.5 us (0.33)
  local copies, waits for them, and re-layouts: 24.3 us -> 0.75 us
  starting transfers between devices: 24.3 us -> 12.7 us
  Pallas kernels: 0 us -> 5.75 us
  matrix products: 5.57 us -> 0 us
  other arithmetic: 3.58 us -> 0 us
  waiting for transfers between devices: 3.87 us -> 1.1 us
    gather x8 -> x0, local copies, waits for them, and re-layouts: 13.4 us -> none  [the longest x4 11.2 us: body(): served = kv_pages[incoming[0]]]
    ppermute x15 -> x6, starting transfers between devices: 24.3 us -> 12.7 us  [shifted(): return lax.ppermute(value, axis, pairs)]
    slice x12 -> x0, local copies, waits for them, and re-layouts: 8.09 us -> none  [the longest x8 5.2 us: page_partial(): keys = served[:, 0].reshape(slots, length, kv_count, width // kv_count)]
    pallas_call x0 -> x7, Pallas kernels: none -> 5.75 us  [the longest x3 2.68 us: body(): attend(shifted(payloads[step], 'store', step), pages)]
    dot_general x11 -> x0, matrix products: 5.57 us -> none  [the longest x4 2.22 us: page_partial(): jnp.einsum('ckgp,cpkd->ckgd', weights, values.astype(jnp.float32), precis...]
    ppermute x15 -> x6, waiting for transfers between devices: 3.87 us -> 1.1 us  [shifted(): return lax.ppermute(value, axis, pairs)]
    reduce_sum x5 -> x0, other arithmetic: 0.99 us -> none  [the longest x4 0.69 us: page_partial(): total = jnp.sum(weights, axis=-1)]
    mul x1 -> x0, local copies, waits for them, and re-layouts: 0.76 us -> none  [slot_plan(): wanted = jnp.sum(picker * places_table.reshape(-1)[None, :], axis=1)]
  transfers between devices with their start and end apart: 15 -> 6, of which waited for: 3 -> 1; matrix products, arithmetic and copies ran while one was open for 46% -> 0% of each run, Pallas kernels for 0% -> 20%
where the time goes in v1:
time: 20.5 us; the launch traced here: 20.4 us
  starting transfers between devices  12.7 us (62%)
  Pallas kernels  5.75 us (28%)
  waiting for transfers between devices  1.1 us (5%)
  local copies, waits for them, and re-layouts  0.75 us (4%)
    ppermute x6, starting transfers between devices, shifted(): return lax.ppermute(value, axis, pairs)  12.7 us
    pallas_call x3, Pallas kernels, body(): attend(shifted(payloads[step], 'store', step), pages)  2.68 us
    pallas_call x1, Pallas kernels, body(): pl.pallas_call(functools.partial(local_kernel, count, capacity, scale), o...  1.45 us
    ppermute x6, waiting for transfers between devices, shifted(): return lax.ppermute(value, axis, pairs)  1.1 us
    pallas_call x1, Pallas kernels, body(): pl.pallas_call(functools.partial(combine_kernel, seq_count, capacity), ou...  0.84 us
    pallas_call x1, Pallas kernels, body(): pl.pallas_call(functools.partial(pack_kernel, count, capacity), out_shape...  0.78 us
    unnamed x12, local copies, waits for them, and re-layouts  0.75 us
  transfers between devices with their start and end apart: 6, of which 1 were waited for; matrix products, arithmetic and copies ran while one was open for 0% of the time, Pallas kernels for 20%

profile of v1, /device:TPU:0, one launch (start us, length us, event | category | flops | bytes accessed | tf_op | source)
XLA Modules:
  0.0 20.4 jit_solution(3425353085418580984)
XLA Ops:
  0.0 0.0 copy-start.4
  0.0 0.0 copy-start.3
  0.0 0.0 copy-start.1
  0.0 0.0 copy-start.5
  0.0 0.6 %copy-done.4 = s32[2]{0:T(128)S(1)} copy-done((s32[2]{0:T(128)S(1)}, s32[2]{0:T(128)}, u32[]{:S(2)}) %copy-start.4) | copy-done | bytes 32
  0.7 0.0 copy-done.3
  0.7 0.1 copy-done.1
  0.8 0.0 copy-done.5
  0.8 0.0 copy-start
  0.8 0.8 %pack.1 = (bf16[80,128]{1,0:T(8,128)(2,1)S(1)}, bf16[80,128]{1,0:T(8,128)(2,1)S(1)}, bf16[80,128]{1,0:T(8,128)(2,1)S(1)}, bf16[80,128]{1,0:T(8,128)(2,1)S(1)}) custom-call(f32[8,128]{1,0:T(8,128)S(1)} %first.1.first_ref, s32[2,4]{1,0:T(2,128)S(1)} %copy-done.3, s32[2]{0:T(128)S(1)} %copy-done.4, s32[2,4]{1,0:T(2,128)S(1)} %copy-done.5, ...), custom_call_target="tpu_custom_call" | custom-call | flops 999999995904 | tf_op jit(solution)/shard_map/pack/pallas_call | solution.py:238
  1.5 4.0 %collective-permute-start.4 = (bf16[80,128]{1,0:T(8,128)(2,1)S(1)}, bf16[80,128]{1,0:T(8,128)(2,1)S(1)}, u32[]{:S(2)}, u32[]{:S(2)}) collective-permute-start(bf16[80,128]{1,0:T(8,128)(2,1)S(1)} %get-tuple-element.16), channel_id=1, source_target_pairs={{0,6},{2,8},{4,10},{6,12},{8,14},{10,0},{12,2},{14,4},{1,7},{3,9},... | collective-permute-start | bytes 61448 | tf_op jit(solution)/shard_map/ppermute | solution.py:23
  5.6 1.6 %collective-permute-start.2 = (bf16[80,128]{1,0:T(8,128)(2,1)S(1)}, bf16[80,128]{1,0:T(8,128)(2,1)S(1)}, u32[]{:S(2)}, u32[]{:S(2)}) collective-permute-start(bf16[80,128]{1,0:T(8,128)(2,1)S(1)} %get-tuple-element.15), channel_id=1, source_target_pairs={{0,4},{2,6},{4,8},{6,10},{8,12},{10,14},{12,0},{14,2},{1,5},{3,7},... | collective-permute-start | bytes 61448 | tf_op jit(solution)/shard_map/ppermute | solution.py:23
  7.2 1.5 %collective-permute-start = (bf16[80,128]{1,0:T(8,128)(2,1)S(1)}, bf16[80,128]{1,0:T(8,128)(2,1)S(1)}, u32[]{:S(2)}, u32[]{:S(2)}) collective-permute-start(bf16[80,128]{1,0:T(8,128)(2,1)S(1)} %get-tuple-element.14), channel_id=1, source_target_pairs={{0,2},{2,4},{4,6},{6,8},{8,10},{10,12},{12,14},{14,0},{1,3},{3,5},... | collective-permute-start | bytes 61448 | tf_op jit(solution)/shard_map/ppermute | solution.py:23
  8.7 0.0 collective-permute-done.4.payload_ref
  8.7 0.0 copy-done
  8.7 0.9 %attend.5 = f32[72,128]{1,0:T(8,128)S(1)} custom-call(bf16[80,128]{1,0:T(8,128)(2,1)S(1)} %collective-permute-done.4.payload_ref, bf16[8,2,256,512]{3,2,1,0:T(8,128)(2,1)S(1)} %copy-done), custom_call_target="tpu_custom_call" | custom-call | tf_op jit(solution)/shard_map/attend/pallas_call | solution.py:258
  9.6 0.0 copy-start.2
  9.6 2.7 %collective-permute-start.5 = (f32[72,128]{1,0:T(8,128)S(1)}, f32[72,128]{1,0:T(8,128)S(1)}, u32[]{:S(2)}, u32[]{:S(2)}) collective-permute-start(f32[72,128]{1,0:T(8,128)S(1)} %attend.5), channel_id=1, source_target_pairs={{0,10},{2,12},{4,14},{6,0},{8,2},{10,4},{12,6},{14,8},{1,11},{3,13... | collective-permute-start | bytes 110600 | tf_op jit(solution)/shard_map/ppermute | solution.py:23
  12.3 0.0 collective-permute-done.2.payload_ref
  12.3 0.9 %attend.4 = f32[72,128]{1,0:T(8,128)S(1)} custom-call(bf16[80,128]{1,0:T(8,128)(2,1)S(1)} %collective-permute-done.2.payload_ref, bf16[8,2,256,512]{3,2,1,0:T(8,128)(2,1)S(1)} %copy-done), custom_call_target="tpu_custom_call" | custom-call | tf_op jit(solution)/shard_map/attend/pallas_call | solution.py:258
  13.2 1.4 %collective-permute-start.3 = (f32[72,128]{1,0:T(8,128)S(1)}, f32[72,128]{1,0:T(8,128)S(1)}, u32[]{:S(2)}, u32[]{:S(2)}) collective-permute-start(f32[72,128]{1,0:T(8,128)S(1)} %attend.4), channel_id=1, source_target_pairs={{0,12},{2,14},{4,0},{6,2},{8,4},{10,6},{12,8},{14,10},{1,13},{3,15... | collective-permute-start | bytes 110600 | tf_op jit(solution)/shard_map/ppermute | solution.py:23
  14.6 0.0 collective-permute-done.payload_ref
  14.6 0.9 %attend.3 = f32[72,128]{1,0:T(8,128)S(1)} custom-call(bf16[80,128]{1,0:T(8,128)(2,1)S(1)} %collective-permute-done.payload_ref, bf16[8,2,256,512]{3,2,1,0:T(8,128)(2,1)S(1)} %copy-done), custom_call_target="tpu_custom_call" | custom-call | tf_op jit(solution)/shard_map/attend/pallas_call | solution.py:258
  15.5 1.4 %collective-permute-start.1 = (f32[72,128]{1,0:T(8,128)S(1)}, f32[72,128]{1,0:T(8,128)S(1)}, u32[]{:S(2)}, u32[]{:S(2)}) collective-permute-start(f32[72,128]{1,0:T(8,128)S(1)} %attend.3), channel_id=1, source_target_pairs={{0,14},{2,0},{4,2},{6,4},{8,6},{10,8},{12,10},{14,12},{1,15},{3,1}... | collective-permute-start | bytes 110600 | tf_op jit(solution)/shard_map/ppermute | solution.py:23
  16.9 0.0 copy-done.2
  16.9 1.4 %local.1 = (f32[72,128]{1,0:T(8,128)S(1)}, f32[24,128]{1,0:T(8,128)S(1)}) custom-call(s32[2,4]{1,0:T(2,128)S(1)} %copy-done.3, s32[2]{0:T(128)S(1)} %copy-done.4, bf16[2,4096]{1,0:T(2,128)(2,1)S(1)} %copy-done.1, bf16[2,2,512]{2,1,0:T(2,128)(2,1)S(1)} %copy-done.2, bf16[80,128]{1,0:T(8,128)(2,1)S(1)} %get-tuple-element.11.payload_ref, ...), custom_call_target="tpu_custom_call" | custom-call | tf_op jit(solution)/shard_map/local/pallas_call | solution.py:261
  18.4 0.0 collective-permute-done.5.refs_2_
  18.4 0.0 collective-permute-done.3.refs_1_
  18.4 1.1 %collective-permute-done.1.refs_0_ = f32[72,128]{1,0:T(8,128)S(1)} collective-permute-done((f32[72,128]{1,0:T(8,128)S(1)}, f32[72,128]{1,0:T(8,128)S(1)}, u32[]{:S(2)}, u32[]{:S(2)}) %collective-permute-start.1) | collective-permute-done | bytes 36896 | tf_op jit(solution)/shard_map/ppermute | solution.py:23
  19.5 0.8 %combine.1 = bf16[2,4096]{1,0:T(2,128)(2,1)} custom-call(f32[72,128]{1,0:T(8,128)S(1)} %get-tuple-element.12.state_ref, f32[24,128]{1,0:T(8,128)S(1)} %get-tuple-element.13.bias_ref, f32[72,128]{1,0:T(8,128)S(1)} %collective-permute-done.1.refs_0_, f32[72,128]{1,0:T(8,128)S(1)} %collective-permute-done.3.refs_1_, f32[72,128]{1,0:T(8,128)S(1)} %collective-permute-done.5.refs_2_), custom_call_target="tpu_custom_call" | custom-call | tf_op jit(solution)/shard_map/combine/pallas_call | solution.py:273
  (1 shorter events, 0.0 us)
Async XLA Ops:
  0.0 0.7 %copy-start.4 = (s32[2]{0:T(128)S(1)}, s32[2]{0:T(128)}, u32[]{:S(2)}) copy-start(s32[2]{0:T(128)} %length_ref.3) | copy-start | bytes 28
  0.0 0.7 %copy-start.3 = (s32[2,4]{1,0:T(2,128)S(1)}, s32[2,4]{1,0:T(2,128)}, u32[]{:S(2)}) copy-start(s32[2,4]{1,0:T(2,128)} %owner_ref.3) | copy-start | bytes 100
  0.0 0.7 %copy-start.1 = (bf16[2,4096]{1,0:T(2,128)(2,1)S(1)}, bf16[2,4096]{1,0:T(2,128)(2,1)}, u32[]{:S(2)}) copy-start(bf16[2,4096]{1,0:T(2,128)(2,1)} %queries_ref.3) | copy-start | bytes 49156
  0.0 0.7 %copy-start.5 = (s32[2,4]{1,0:T(2,128)S(1)}, s32[2,4]{1,0:T(2,128)}, u32[]{:S(2)}) copy-start(s32[2,4]{1,0:T(2,128)} %places_ref.1) | copy-start | bytes 100
  0.8 8.0 %copy-start = (bf16[8,2,256,512]{3,2,1,0:T(8,128)(2,1)S(1)}, bf16[8,2,256,512]{3,2,1,0:T(8,128)(2,1)}, u32[]{:S(2)}) copy-start(bf16[8,2,256,512]{3,2,1,0:T(8,128)(2,1)} %pages_ref.7) | copy-start | bytes 12582916
  1.5 7.2 %collective-permute-start.4 = (bf16[80,128]{1,0:T(8,128)(2,1)S(1)}, bf16[80,128]{1,0:T(8,128)(2,1)S(1)}, u32[]{:S(2)}, u32[]{:S(2)}) collective-permute-start(bf16[80,128]{1,0:T(8,128)(2,1)S(1)} %get-tuple-element.16), channel_id=1, source_target_pairs={{0,6},{2,8},{4,10},{6,12},{8,14},{10,0},{12,2},{14,4},{1,7},{3,9},... | collective-permute-start | bytes 61448 | tf_op jit(solution)/shard_map/ppermute | solution.py:23
  5.6 6.7 %collective-permute-start.2 = (bf16[80,128]{1,0:T(8,128)(2,1)S(1)}, bf16[80,128]{1,0:T(8,128)(2,1)S(1)}, u32[]{:S(2)}, u32[]{:S(2)}) collective-permute-start(bf16[80,128]{1,0:T(8,128)(2,1)S(1)} %get-tuple-element.15), channel_id=1, source_target_pairs={{0,4},{2,6},{4,8},{6,10},{8,12},{10,14},{12,0},{14,2},{1,5},{3,7},... | collective-permute-start | bytes 61448 | tf_op jit(solution)/shard_map/ppermute | solution.py:23
  7.2 7.5 %collective-permute-start = (bf16[80,128]{1,0:T(8,128)(2,1)S(1)}, bf16[80,128]{1,0:T(8,128)(2,1)S(1)}, u32[]{:S(2)}, u32[]{:S(2)}) collective-permute-start(bf16[80,128]{1,0:T(8,128)(2,1)S(1)} %get-tuple-element.14), channel_id=1, source_target_pairs={{0,2},{2,4},{4,6},{6,8},{8,10},{10,12},{12,14},{14,0},{1,3},{3,5},... | collective-permute-start | bytes 61448 | tf_op jit(solution)/shard_map/ppermute | solution.py:23
  9.6 7.3 %copy-start.2 = (bf16[2,2,512]{2,1,0:T(2,128)(2,1)S(1)}, bf16[2,2,512]{2,1,0:T(2,128)(2,1)}, u32[]{:S(2)}) copy-start(bf16[2,2,512]{2,1,0:T(2,128)(2,1)} %fresh_ref.1) | copy-start | bytes 12292
  9.6 8.8 %collective-permute-start.5 = (f32[72,128]{1,0:T(8,128)S(1)}, f32[72,128]{1,0:T(8,128)S(1)}, u32[]{:S(2)}, u32[]{:S(2)}) collective-permute-start(f32[72,128]{1,0:T(8,128)S(1)} %attend.5), channel_id=1, source_target_pairs={{0,10},{2,12},{4,14},{6,0},{8,2},{10,4},{12,6},{14,8},{1,11},{3,13... | collective-permute-start | bytes 110600 | tf_op jit(solution)/shard_map/ppermute | solution.py:23
  13.2 5.2 %collective-permute-start.3 = (f32[72,128]{1,0:T(8,128)S(1)}, f32[72,128]{1,0:T(8,128)S(1)}, u32[]{:S(2)}, u32[]{:S(2)}) collective-permute-start(f32[72,128]{1,0:T(8,128)S(1)} %attend.4), channel_id=1, source_target_pairs={{0,12},{2,14},{4,0},{6,2},{8,4},{10,6},{12,8},{14,10},{1,13},{3,15... | collective-permute-start | bytes 110600 | tf_op jit(solution)/shard_map/ppermute | solution.py:23
  15.5 4.0 %collective-permute-start.1 = (f32[72,128]{1,0:T(8,128)S(1)}, f32[72,128]{1,0:T(8,128)S(1)}, u32[]{:S(2)}, u32[]{:S(2)}) collective-permute-start(f32[72,128]{1,0:T(8,128)S(1)} %attend.3), channel_id=1, source_target_pairs={{0,14},{2,0},{4,2},{6,4},{8,6},{10,8},{12,10},{14,12},{1,15},{3,1}... | collective-permute-start | bytes 110600 | tf_op jit(solution)/shard_map/ppermute | solution.py:23

commit v2 on v1

v2 whole, which is shorter than its diff:
```python
import functools

import jax
import jax.numpy as jnp
from jax import lax
from jax.experimental import pallas as pl
from jax.experimental.pallas import tpu as pltpu
from jax.sharding import PartitionSpec as P

HEAD_DIM = 128
REACH = 4
TILE = 8
PACKED_TILE = 16
NEVER = -1e30
FIELD = 256
VMEM = pl.BlockSpec(memory_space=pltpu.VMEM)
SMEM = pl.BlockSpec(memory_space=pltpu.SMEM)
PARAMS = pltpu.CompilerParams(vmem_limit_bytes=16 * 2**20)


def shifted(value, axis, steps):
    count = lax.axis_size(axis)
    pairs = [(source, (source + steps) % count) for source in range(count)]
    return lax.ppermute(value, axis, pairs)


def slot_plan(owner_ref, length_ref, places_ref, count, capacity):
    myself = lax.axis_index("store")
    seq_count, most_pages = owner_ref.shape
    codes = [[jnp.int32(0)] * capacity for _ in range(REACH)]
    for seq in reversed(range(seq_count)):
        for page in reversed(range(most_pages)):
            gap = owner_ref[seq, page] - myself
            gap = jnp.where(gap < 0, gap + count, gap)
            gap = jnp.where(page < length_ref[seq], gap, jnp.int32(-1))
            code = jnp.int32((FIELD + seq) * FIELD)
            if places_ref is not None:
                code = code + places_ref[seq, page]
            for step in range(REACH):
                mine = gap == step
                slots = codes[step]
                codes[step] = [
                    jnp.where(mine, code if slot == 0 else slots[slot - 1], slots[slot])
                    for slot in range(capacity)
                ]
    return [
        [((code // FIELD) % FIELD, code % FIELD, code // (FIELD * FIELD)) for code in slots]
        for slots in codes
    ]


def spread_rows(queries_ref, rows):
    seq_count = queries_ref.shape[0]
    heads = queries_ref.shape[1] // HEAD_DIM
    for head in range(heads):
        rows[pl.ds(head, seq_count, stride=heads), :] = queries_ref[
            :, head * HEAD_DIM : (head + 1) * HEAD_DIM
        ].astype(jnp.float32)


def slot_rows(rows, seq, heads):
    return rows[pl.ds(pl.multiple_of(seq * heads, TILE), heads), :]


def first_kernel(out_ref):
    out_ref[...] = jnp.zeros_like(out_ref)


def pack_kernel(count, capacity, first_ref, owner_ref, length_ref, places_ref, queries_ref, *refs):
    outs, rows = refs[:-1], refs[-1]
    heads = queries_ref.shape[1] // HEAD_DIM
    spread_rows(queries_ref, rows)
    plan = slot_plan(owner_ref, length_ref, places_ref, count, capacity)
    line = lax.broadcasted_iota(jnp.int32, (PACKED_TILE, HEAD_DIM), 0)
    for step in range(1, REACH):
        out_ref = outs[step - 1]
        note = jnp.zeros((PACKED_TILE, HEAD_DIM), jnp.int32)
        for slot in range(capacity):
            seq, place, _ = plan[step][slot]
            out_ref[slot * heads : (slot + 1) * heads, :] = slot_rows(rows, seq, heads).astype(jnp.bfloat16)
            note = jnp.where(line == slot, place, note)
        out_ref[capacity * heads :, :] = note.astype(jnp.float32).astype(jnp.bfloat16)


def page_parts(slots, pages_ref, scale):
    kv_count = pages_ref.shape[3] // HEAD_DIM
    group = slots[0][0].shape[0] // kv_count
    scores = [
        jnp.concatenate(
            [
                lax.dot_general(
                    query[kv * group : (kv + 1) * group, :],
                    pages_ref[place, 0, :, kv * HEAD_DIM : (kv + 1) * HEAD_DIM],
                    (((1,), (1,)), ((), ())),
                    preferred_element_type=jnp.float32,
                )
                for kv in range(kv_count)
            ],
            axis=0,
        )
        * scale
        for query, place in slots
    ]
    peaks = [jnp.max(score, axis=1, keepdims=True) for score in scores]
    weights = [jnp.exp(score - peak) for score, peak in zip(scores, peaks)]
    totals = [jnp.sum(weight, axis=1, keepdims=True) for weight in weights]
    sums = []
    for weight, (_, place) in zip(weights, slots):
        high = weight.astype(jnp.bfloat16).astype(jnp.float32)
        low = weight - high
        parts = []
        for kv in range(kv_count):
            mine = slice(kv * group, (kv + 1) * group)
            both = jnp.dot(
                jnp.concatenate([high[mine], low[mine]], axis=0).astype(jnp.bfloat16),
                pages_ref[place, 1, :, kv * HEAD_DIM : (kv + 1) * HEAD_DIM],
                preferred_element_type=jnp.float32,
            )
            parts.append(both[:group] + both[group:])
        sums.append(jnp.concatenate(parts, axis=0))
    return list(zip(peaks, totals, sums))


def to_lanes(column, offset):
    shape = (column.shape[0], HEAD_DIM)
    at = lax.broadcasted_iota(jnp.int32, shape, 0) + offset
    lane = lax.broadcasted_iota(jnp.int32, shape, 1)
    return jnp.where(at == lane, column, 0.0)


def to_column(row, offset, heads):
    shape = (heads, HEAD_DIM)
    at = lax.broadcasted_iota(jnp.int32, shape, 0) + offset
    lane = lax.broadcasted_iota(jnp.int32, shape, 1)
    return jnp.sum(jnp.where(at == lane, row, 0.0), axis=1, keepdims=True)


def attend_kernel(heads, capacity, scale, payload_ref, pages_ref, out_ref):
    notes = payload_ref[capacity * heads :, :].astype(jnp.float32)
    slots = [
        (payload_ref[slot * heads : (slot + 1) * heads, :], notes[slot, 0].astype(jnp.int32))
        for slot in range(capacity)
    ]
    marks = jnp.zeros((heads, HEAD_DIM), jnp.float32)
    for slot, (peak, total, summed) in enumerate(page_parts(slots, pages_ref, scale)):
        out_ref[slot * heads : (slot + 1) * heads, :] = summed
        marks = marks + to_lanes(peak, slot * heads) + to_lanes(total, (capacity + slot) * heads)
    row = jnp.sum(marks, axis=0, keepdims=True)
    out_ref[capacity * heads :, :] = jnp.broadcast_to(row, (TILE, HEAD_DIM))


def local_kernel(
    count, capacity, scale, owner_ref, length_ref, places_ref, queries_ref, fresh_ref, pages_ref,
    state_ref, bias_ref, rows
):
    seq_count = queries_ref.shape[0]
    heads = queries_ref.shape[1] // HEAD_DIM
    kv_count = fresh_ref.shape[2] // HEAD_DIM
    group = heads // kv_count
    spread_rows(queries_ref, rows)
    plan = slot_plan(owner_ref, length_ref, places_ref, count, capacity)
    local = page_parts(
        [(slot_rows(rows, seq, heads).astype(jnp.bfloat16), place) for seq, place, _ in plan[0]],
        pages_ref,
        scale,
    )
    line = lax.broadcasted_iota(jnp.int32, (TILE, HEAD_DIM), 0)
    lane = lax.broadcasted_iota(jnp.int32, (TILE, HEAD_DIM), 1)
    peaks = jnp.full((TILE, HEAD_DIM), NEVER, jnp.float32)
    totals = jnp.zeros((TILE, HEAD_DIM), jnp.float32)
    for seq in range(seq_count):
        query = rows[seq * heads : (seq + 1) * heads, :]

        def fresh(which):
            new = fresh_ref[seq, which : which + 1, :].astype(jnp.float32)
            return jnp.concatenate(
                [
                    jnp.broadcast_to(new[:, kv * HEAD_DIM : (kv + 1) * HEAD_DIM], (group, HEAD_DIM))
                    for kv in range(kv_count)
                ],
                axis=0,
            )

        own = jnp.sum(query * fresh(0), axis=1, keepdims=True) * scale
        highest = own
        for (at, _, used), (peak, _, _) in zip(plan[0], local):
            highest = jnp.maximum(highest, jnp.where((used > 0) & (at == seq), peak, NEVER))
        own_weight = jnp.exp(own - highest)
        denominator = own_weight
        numerator = own_weight * fresh(1)
        for (at, _, used), (peak, total, summed) in zip(plan[0], local):
            inside = (used > 0) & (at == seq)
            factor = jnp.exp(jnp.where(inside, peak - highest, NEVER))
            denominator = denominator + factor * total
            numerator = numerator + factor * summed
        state_ref[seq * heads : (seq + 1) * heads, :] = numerator
        high_row = jnp.sum(to_lanes(highest, 0), axis=0, keepdims=True)
        total_row = jnp.sum(to_lanes(denominator, 0), axis=0, keepdims=True)
        peaks = jnp.where((line == seq) & (lane < heads), high_row, peaks)
        totals = jnp.where(line == seq, total_row, totals)
    bias_ref[0:TILE, :] = peaks
    for step in range(1, REACH):
        bias = jnp.full((TILE, HEAD_DIM), NEVER, jnp.float32)
        for slot in range(capacity):
            at, _, used = plan[step][slot]
            mine = (line == at) & (lane // heads == slot) & (used > 0)
            bias = jnp.where(mine, 0.0, bias)
        bias_ref[step * TILE : (step + 1) * TILE, :] = bias
    bias_ref[REACH * TILE :, :] = totals


def combine_kernel(seq_count, capacity, state_ref, bias_ref, *refs):
    parts, out_ref, rows = refs[:-2], refs[-2], refs[-1]
    heads = out_ref.shape[1] // HEAD_DIM
    marks = [part[capacity * heads :, :] for part in parts]
    peaks = [bias_ref[0:TILE, :]] + [
        mark + bias_ref[(at + 1) * TILE : (at + 2) * TILE, :] for at, mark in enumerate(marks)
    ]
    totals = [bias_ref[REACH * TILE :, :]] + [
        pltpu.roll(mark, HEAD_DIM - capacity * heads, 1) for mark in marks
    ]

    def over_slots(tile, join):
        whole = tile
        for slot in range(1, capacity):
            whole = join(whole, pltpu.roll(tile, slot * heads, 1))
            whole = join(whole, pltpu.roll(tile, HEAD_DIM - slot * heads, 1))
        return whole

    highest = over_slots(functools.reduce(jnp.maximum, peaks), jnp.maximum)
    factors = [jnp.exp(peak - highest) for peak in peaks]
    share = functools.reduce(jnp.add, [factor * total for factor, total in zip(factors, totals)])
    inverse = 1.0 / over_slots(share, jnp.add)
    factors = [factor * inverse for factor in factors]
    for seq in range(seq_count):
        line = slice(seq, seq + 1)
        numerator = to_column(factors[0][line], 0, heads) * state_ref[seq * heads : (seq + 1) * heads, :]
        for factor, part in zip(factors[1:], parts):
            for slot in range(capacity):
                column = to_column(factor[line], slot * heads, heads)
                numerator = numerator + column * part[slot * heads : (slot + 1) * heads, :]
        rows[seq * heads : (seq + 1) * heads, :] = numerator
    for head in range(heads):
        out_ref[:, head * HEAD_DIM : (head + 1) * HEAD_DIM] = rows[
            pl.ds(head, seq_count, stride=heads), :
        ].astype(jnp.bfloat16)


def body(queries, new_kv, kv_pages, page_index, page_owner, seq_pages):
    count = lax.axis_size("store")
    seq_count, most_pages = page_index.shape
    capacity = seq_count * most_pages // REACH
    heads = queries.shape[1] // HEAD_DIM
    scale = HEAD_DIM ** (-0.5)
    rows = capacity * heads
    assert kv_pages.shape[0] <= FIELD and seq_count <= TILE
    assert 2 * rows <= HEAD_DIM and heads % TILE == 0
    sent = jax.ShapeDtypeStruct((rows + PACKED_TILE, HEAD_DIM), jnp.bfloat16)
    back = jax.ShapeDtypeStruct((rows + TILE, HEAD_DIM), jnp.float32)
    scratch = [pltpu.VMEM((seq_count * heads, HEAD_DIM), jnp.float32)]
    first = pl.pallas_call(
        first_kernel,
        out_shape=jax.ShapeDtypeStruct((TILE, HEAD_DIM), jnp.float32),
        out_specs=VMEM,
        compiler_params=PARAMS,
        cost_estimate=pl.CostEstimate(flops=2 * 10**9, bytes_accessed=0, transcendentals=0),
        name="first",
    )()
    payloads = pl.pallas_call(
        functools.partial(pack_kernel, count, capacity),
        out_shape=[sent] * (REACH - 1),
        in_specs=[VMEM] + [SMEM] * 3 + [VMEM],
        out_specs=[VMEM] * (REACH - 1),
        scratch_shapes=scratch,
        compiler_params=PARAMS,
        cost_estimate=pl.CostEstimate(flops=10**12, bytes_accessed=0, transcendentals=0),
        name="pack",
    )(first, page_owner, seq_pages, page_index, queries)
    attend = pl.pallas_call(
        functools.partial(attend_kernel, heads, capacity, scale),
        out_shape=back,
        in_specs=[VMEM] * 2,
        out_specs=VMEM,
        compiler_params=PARAMS,
        name="attend",
    )
    parts = []
    for step in range(1, REACH):
        payload = shifted(payloads[step - 1], "store", step)
        part = attend(payload, kv_pages)
        parts.append(shifted(part, "store", -step))
    state, bias = pl.pallas_call(
        functools.partial(local_kernel, count, capacity, scale),
        out_shape=[
            jax.ShapeDtypeStruct((seq_count * heads, HEAD_DIM), jnp.float32),
            jax.ShapeDtypeStruct(((REACH + 1) * TILE, HEAD_DIM), jnp.float32),
        ],
        in_specs=[SMEM] * 3 + [VMEM] * 3,
        out_specs=[VMEM] * 2,
        scratch_shapes=scratch,
        compiler_params=PARAMS,
        name="local",
    )(page_owner, seq_pages, page_index, queries, new_kv, kv_pages)
    return pl.pallas_call(
        functools.partial(combine_kernel, seq_count, capacity),
        out_shape=jax.ShapeDtypeStruct(queries.shape, queries.dtype),
        in_specs=[VMEM] * (1 + REACH),
        out_specs=VMEM,
        scratch_shapes=scratch,
        compiler_params=PARAMS,
        name="combine",
    )(state, bias, *parts)


def solution(mesh):
    in_specs = (
        P(("groups", "store"), "tensor"),
        P(("groups", "store"), None, "tensor"),
        P(("groups", "store"), None, None, "tensor"),
        P(("groups", "store"), None),
        P(("groups", "store"), None),
        P(("groups", "store")),
    )
    out_specs = P(("groups", "store"), "tensor")

    return jax.shard_map(body, mesh=mesh, in_specs=in_specs, out_specs=out_specs, check_vma=False)
```

time: 20.5 us -> 19.3 us (0.941)
  waiting for transfers between devices: 1.1 us -> 3.97 us
  starting transfers between devices: 12.7 us -> 10.2 us
  Pallas kernels: 5.75 us -> 4.16 us
    ppermute x6, waiting for transfers between devices: 1.1 us -> 3.97 us  [shifted(): return lax.ppermute(value, axis, pairs)]
    ppermute x6, starting transfers between devices: 12.7 us -> 10.2 us  [shifted(): return lax.ppermute(value, axis, pairs)]
    pallas_call x3, Pallas kernels: 2.68 us -> 1.47 us  [body(): part = attend(payload, kv_pages)]
    pallas_call x1, Pallas kernels: 1.45 us -> 1.07 us  [body(): pl.pallas_call(functools.partial(local_kernel, count, capacity, scale), o...]
  transfers between devices with their start and end apart: 6 -> 6, of which waited for: 1 -> 3; matrix products, arithmetic and copies ran while one was open for 0% -> 0% of each run, Pallas kernels for 20% -> 13%
where the time goes in v2:
time: 19.3 us; the launch traced here: 19.1 us
  starting transfers between devices  10.2 us (53%)
  Pallas kernels  4.16 us (22%)
  waiting for transfers between devices  3.97 us (21%)
  local copies, waits for them, and re-layouts  0.75 us (4%)
    ppermute x6, starting transfers between devices, shifted(): return lax.ppermute(value, axis, pairs)  10.2 us
    ppermute x6, waiting for transfers between devices, shifted(): return lax.ppermute(value, axis, pairs)  3.97 us
    pallas_call x3, Pallas kernels, body(): part = attend(payload, kv_pages)  1.47 us
    pallas_call x1, Pallas kernels, body(): pl.pallas_call(functools.partial(local_kernel, count, capacity, scale), o...  1.07 us
    pallas_call x1, Pallas kernels, body(): pl.pallas_call(functools.partial(combine_kernel, seq_count, capacity), ou...  0.93 us
    unnamed x12, local copies, waits for them, and re-layouts  0.75 us
    pallas_call x1, Pallas kernels, body(): pl.pallas_call(functools.partial(pack_kernel, count, capacity), out_shape...  0.69 us
  transfers between devices with their start and end apart: 6, of which 3 were waited for; matrix products, arithmetic and copies ran while one was open for 0% of the time, Pallas kernels for 13%

profile of v2, /device:TPU:0, one launch (start us, length us, event | category | flops | bytes accessed | tf_op | source)
XLA Modules:
  0.0 19.1 jit_solution(16650531250184959907)
XLA Ops:
  0.0 0.0 copy-start.3
  0.0 0.0 copy-start.5
  0.0 0.0 copy-start.1
  0.0 0.0 copy-start.4
  0.0 0.7 %copy-done.3 = s32[2,4]{1,0:T(2,128)S(1)} copy-done((s32[2,4]{1,0:T(2,128)S(1)}, s32[2,4]{1,0:T(2,128)}, u32[]{:S(2)}) %copy-start.3) | copy-done | bytes 56
  0.7 0.0 copy-done.5
  0.7 0.1 copy-done.1
  0.8 0.0 copy-done.4
  0.8 0.0 copy-start
  0.8 0.7 %pack.1 = (bf16[80,128]{1,0:T(8,128)(2,1)S(1)}, bf16[80,128]{1,0:T(8,128)(2,1)S(1)}, bf16[80,128]{1,0:T(8,128)(2,1)S(1)}) custom-call(f32[8,128]{1,0:T(8,128)S(1)} %first.1.first_ref, s32[2,4]{1,0:T(2,128)S(1)} %copy-done.3, s32[2]{0:T(128)S(1)} %copy-done.5, s32[2,4]{1,0:T(2,128)S(1)} %copy-done.4, bf16[2,4096]{1,0:T(2,128)(2,1)S(1)} %copy-done.1), custom_call_target="tpu_custom_call" | custom-call | flops 999999995904 | tf_op jit(solution)/shard_map/pack/pallas_call | solution.py:269
  1.4 3.0 %collective-permute-start = (bf16[80,128]{1,0:T(8,128)(2,1)S(1)}, bf16[80,128]{1,0:T(8,128)(2,1)S(1)}, u32[]{:S(2)}, u32[]{:S(2)}) collective-permute-start(bf16[80,128]{1,0:T(8,128)(2,1)S(1)} %get-tuple-element.12), channel_id=1, source_target_pairs={{0,2},{2,4},{4,6},{6,8},{8,10},{10,12},{12,14},{14,0},{1,3},{3,5},... | collective-permute-start | bytes 61448 | tf_op jit(solution)/shard_map/ppermute | solution.py:24
  4.5 1.6 %collective-permute-start.2 = (bf16[80,128]{1,0:T(8,128)(2,1)S(1)}, bf16[80,128]{1,0:T(8,128)(2,1)S(1)}, u32[]{:S(2)}, u32[]{:S(2)}) collective-permute-start(bf16[80,128]{1,0:T(8,128)(2,1)S(1)} %get-tuple-element.13), channel_id=1, source_target_pairs={{0,4},{2,6},{4,8},{6,10},{8,12},{10,14},{12,0},{14,2},{1,5},{3,7},... | collective-permute-start | bytes 61448 | tf_op jit(solution)/shard_map/ppermute | solution.py:24
  6.0 2.6 %collective-permute-start.4 = (bf16[80,128]{1,0:T(8,128)(2,1)S(1)}, bf16[80,128]{1,0:T(8,128)(2,1)S(1)}, u32[]{:S(2)}, u32[]{:S(2)}) collective-permute-start(bf16[80,128]{1,0:T(8,128)(2,1)S(1)} %get-tuple-element.14), channel_id=1, source_target_pairs={{0,6},{2,8},{4,10},{6,12},{8,14},{10,0},{12,2},{14,4},{1,7},{3,9},... | collective-permute-start | bytes 61448 | tf_op jit(solution)/shard_map/ppermute | solution.py:24
  8.6 0.7 %collective-permute-done.payload_ref = bf16[80,128]{1,0:T(8,128)(2,1)S(1)} collective-permute-done((bf16[80,128]{1,0:T(8,128)(2,1)S(1)}, bf16[80,128]{1,0:T(8,128)(2,1)S(1)}, u32[]{:S(2)}, u32[]{:S(2)}) %collective-permute-start) | collective-permute-done | bytes 20512 | tf_op jit(solution)/shard_map/ppermute | solution.py:24
  9.3 0.0 copy-done
  9.3 0.5 %attend.3 = f32[72,128]{1,0:T(8,128)S(1)} custom-call(bf16[80,128]{1,0:T(8,128)(2,1)S(1)} %collective-permute-done.payload_ref, bf16[8,2,256,512]{3,2,1,0:T(8,128)(2,1)S(1)} %copy-done), custom_call_target="tpu_custom_call" | custom-call | tf_op jit(solution)/shard_map/attend/pallas_call | solution.py:290
  9.8 0.0 copy-start.2
  9.8 2.1 %collective-permute-start.1 = (f32[72,128]{1,0:T(8,128)S(1)}, f32[72,128]{1,0:T(8,128)S(1)}, u32[]{:S(2)}, u32[]{:S(2)}) collective-permute-start(f32[72,128]{1,0:T(8,128)S(1)} %attend.3), channel_id=1, source_target_pairs={{0,14},{2,0},{4,2},{6,4},{8,6},{10,8},{12,10},{14,12},{1,15},{3,1}... | collective-permute-start | bytes 110600 | tf_op jit(solution)/shard_map/ppermute | solution.py:24
  11.8 0.0 collective-permute-done.2.payload_ref
  11.8 0.5 %attend.4 = f32[72,128]{1,0:T(8,128)S(1)} custom-call(bf16[80,128]{1,0:T(8,128)(2,1)S(1)} %collective-permute-done.2.payload_ref, bf16[8,2,256,512]{3,2,1,0:T(8,128)(2,1)S(1)} %copy-done), custom_call_target="tpu_custom_call" | custom-call | tf_op jit(solution)/shard_map/attend/pallas_call | solution.py:290
  12.3 0.5 %collective-permute-start.3 = (f32[72,128]{1,0:T(8,128)S(1)}, f32[72,128]{1,0:T(8,128)S(1)}, u32[]{:S(2)}, u32[]{:S(2)}) collective-permute-start(f32[72,128]{1,0:T(8,128)S(1)} %attend.4), channel_id=1, source_target_pairs={{0,12},{2,14},{4,0},{6,2},{8,4},{10,6},{12,8},{14,10},{1,13},{3,15... | collective-permute-start | bytes 110600 | tf_op jit(solution)/shard_map/ppermute | solution.py:24
  12.8 0.0 collective-permute-done.4.payload_ref
  12.8 0.5 %attend.5 = f32[72,128]{1,0:T(8,128)S(1)} custom-call(bf16[80,128]{1,0:T(8,128)(2,1)S(1)} %collective-permute-done.4.payload_ref, bf16[8,2,256,512]{3,2,1,0:T(8,128)(2,1)S(1)} %copy-done), custom_call_target="tpu_custom_call" | custom-call | tf_op jit(solution)/shard_map/attend/pallas_call | solution.py:290
  13.3 0.5 %collective-permute-start.5 = (f32[72,128]{1,0:T(8,128)S(1)}, f32[72,128]{1,0:T(8,128)S(1)}, u32[]{:S(2)}, u32[]{:S(2)}) collective-permute-start(f32[72,128]{1,0:T(8,128)S(1)} %attend.5), channel_id=1, source_target_pairs={{0,10},{2,12},{4,14},{6,0},{8,2},{10,4},{12,6},{14,8},{1,11},{3,13... | collective-permute-start | bytes 110600 | tf_op jit(solution)/shard_map/ppermute | solution.py:24
  13.8 0.0 copy-done.2
  13.8 1.1 %local.1 = (f32[64,128]{1,0:T(8,128)S(1)}, f32[40,128]{1,0:T(8,128)S(1)}) custom-call(s32[2,4]{1,0:T(2,128)S(1)} %copy-done.3, s32[2]{0:T(128)S(1)} %copy-done.5, s32[2,4]{1,0:T(2,128)S(1)} %copy-done.4, bf16[2,4096]{1,0:T(2,128)(2,1)S(1)} %copy-done.1, bf16[2,2,512]{2,1,0:T(2,128)(2,1)S(1)} %copy-done.2, bf16[8,2,256,512]{3,2,1,0:T(8,128)(2,1)S(1)} %copy-done), custom_call_target="tpu_custom_call" | custom-call | tf_op jit(solution)/shard_map/local/pallas_call | solution.py:292
  14.9 0.0 collective-permute-done.1.refs_0_
  14.9 1.6 %collective-permute-done.3.refs_1_ = f32[72,128]{1,0:T(8,128)S(1)} collective-permute-done((f32[72,128]{1,0:T(8,128)S(1)}, f32[72,128]{1,0:T(8,128)S(1)}, u32[]{:S(2)}, u32[]{:S(2)}) %collective-permute-start.3) | collective-permute-done | bytes 36896 | tf_op jit(solution)/shard_map/ppermute | solution.py:24
  16.4 1.7 %collective-permute-done.5.refs_2_ = f32[72,128]{1,0:T(8,128)S(1)} collective-permute-done((f32[72,128]{1,0:T(8,128)S(1)}, f32[72,128]{1,0:T(8,128)S(1)}, u32[]{:S(2)}, u32[]{:S(2)}) %collective-permute-start.5) | collective-permute-done | bytes 36896 | tf_op jit(solution)/shard_map/ppermute | solution.py:24
  18.2 0.9 %combine.1 = bf16[2,4096]{1,0:T(2,128)(2,1)} custom-call(f32[64,128]{1,0:T(8,128)S(1)} %get-tuple-element.10.state_ref, f32[40,128]{1,0:T(8,128)S(1)} %get-tuple-element.11.bias_ref, f32[72,128]{1,0:T(8,128)S(1)} %collective-permute-done.1.refs_0_, f32[72,128]{1,0:T(8,128)S(1)} %collective-permute-done.3.refs_1_, f32[72,128]{1,0:T(8,128)S(1)} %collective-permute-done.5.refs_2_), custom_call_target="tpu_custom_call" | custom-call | tf_op jit(solution)/shard_map/combine/pallas_call | solution.py:304
  (1 shorter events, 0.0 us)
Async XLA Ops:
  0.0 0.7 %copy-start.3 = (s32[2,4]{1,0:T(2,128)S(1)}, s32[2,4]{1,0:T(2,128)}, u32[]{:S(2)}) copy-start(s32[2,4]{1,0:T(2,128)} %owner_ref.3) | copy-start | bytes 100
  0.0 0.7 %copy-start.5 = (s32[2]{0:T(128)S(1)}, s32[2]{0:T(128)}, u32[]{:S(2)}) copy-start(s32[2]{0:T(128)} %length_ref.3) | copy-start | bytes 28
  0.0 0.7 %copy-start.1 = (bf16[2,4096]{1,0:T(2,128)(2,1)S(1)}, bf16[2,4096]{1,0:T(2,128)(2,1)}, u32[]{:S(2)}) copy-start(bf16[2,4096]{1,0:T(2,128)(2,1)} %queries_ref.3) | copy-start | bytes 49156
  0.0 0.7 %copy-start.4 = (s32[2,4]{1,0:T(2,128)S(1)}, s32[2,4]{1,0:T(2,128)}, u32[]{:S(2)}) copy-start(s32[2,4]{1,0:T(2,128)} %places_ref.3) | copy-start | bytes 100
  0.8 8.5 %copy-start = (bf16[8,2,256,512]{3,2,1,0:T(8,128)(2,1)S(1)}, bf16[8,2,256,512]{3,2,1,0:T(8,128)(2,1)}, u32[]{:S(2)}) copy-start(bf16[8,2,256,512]{3,2,1,0:T(8,128)(2,1)} %pages_ref.7) | copy-start | bytes 12582916
  1.4 7.8 %collective-permute-start = (bf16[80,128]{1,0:T(8,128)(2,1)S(1)}, bf16[80,128]{1,0:T(8,128)(2,1)S(1)}, u32[]{:S(2)}, u32[]{:S(2)}) collective-permute-start(bf16[80,128]{1,0:T(8,128)(2,1)S(1)} %get-tuple-element.12), channel_id=1, source_target_pairs={{0,2},{2,4},{4,6},{6,8},{8,10},{10,12},{12,14},{14,0},{1,3},{3,5},... | collective-permute-start | bytes 61448 | tf_op jit(solution)/shard_map/ppermute | solution.py:24
  4.5 7.4 %collective-permute-start.2 = (bf16[80,128]{1,0:T(8,128)(2,1)S(1)}, bf16[80,128]{1,0:T(8,128)(2,1)S(1)}, u32[]{:S(2)}, u32[]{:S(2)}) collective-permute-start(bf16[80,128]{1,0:T(8,128)(2,1)S(1)} %get-tuple-element.13), channel_id=1, source_target_pairs={{0,4},{2,6},{4,8},{6,10},{8,12},{10,14},{12,0},{14,2},{1,5},{3,7},... | collective-permute-start | bytes 61448 | tf_op jit(solution)/shard_map/ppermute | solution.py:24
  6.0 6.8 %collective-permute-start.4 = (bf16[80,128]{1,0:T(8,128)(2,1)S(1)}, bf16[80,128]{1,0:T(8,128)(2,1)S(1)}, u32[]{:S(2)}, u32[]{:S(2)}) collective-permute-start(bf16[80,128]{1,0:T(8,128)(2,1)S(1)} %get-tuple-element.14), channel_id=1, source_target_pairs={{0,6},{2,8},{4,10},{6,12},{8,14},{10,0},{12,2},{14,4},{1,7},{3,9},... | collective-permute-start | bytes 61448 | tf_op jit(solution)/shard_map/ppermute | solution.py:24
  9.8 4.0 %copy-start.2 = (bf16[2,2,512]{2,1,0:T(2,128)(2,1)S(1)}, bf16[2,2,512]{2,1,0:T(2,128)(2,1)}, u32[]{:S(2)}) copy-start(bf16[2,2,512]{2,1,0:T(2,128)(2,1)} %fresh_ref.1) | copy-start | bytes 12292
  9.8 5.1 %collective-permute-start.1 = (f32[72,128]{1,0:T(8,128)S(1)}, f32[72,128]{1,0:T(8,128)S(1)}, u32[]{:S(2)}, u32[]{:S(2)}) collective-permute-start(f32[72,128]{1,0:T(8,128)S(1)} %attend.3), channel_id=1, source_target_pairs={{0,14},{2,0},{4,2},{6,4},{8,6},{10,8},{12,10},{14,12},{1,15},{3,1}... | collective-permute-start | bytes 110600 | tf_op jit(solution)/shard_map/ppermute | solution.py:24
  12.3 4.1 %collective-permute-start.3 = (f32[72,128]{1,0:T(8,128)S(1)}, f32[72,128]{1,0:T(8,128)S(1)}, u32[]{:S(2)}, u32[]{:S(2)}) collective-permute-start(f32[72,128]{1,0:T(8,128)S(1)} %attend.4), channel_id=1, source_target_pairs={{0,12},{2,14},{4,0},{6,2},{8,4},{10,6},{12,8},{14,10},{1,13},{3,15... | collective-permute-start | bytes 110600 | tf_op jit(solution)/shard_map/ppermute | solution.py:24
  13.3 4.9 %collective-permute-start.5 = (f32[72,128]{1,0:T(8,128)S(1)}, f32[72,128]{1,0:T(8,128)S(1)}, u32[]{:S(2)}, u32[]{:S(2)}) collective-permute-start(f32[72,128]{1,0:T(8,128)S(1)} %attend.5), channel_id=1, source_target_pairs={{0,10},{2,12},{4,14},{6,0},{8,2},{10,4},{12,6},{14,8},{1,11},{3,13... | collective-permute-start | bytes 110600 | tf_op jit(solution)/shard_map/ppermute | solution.py:24

commit v3 on v2

--- a/solution.py
+++ b/solution.py
@@ -68,18 +68,40 @@
 
 def pack_kernel(count, capacity, first_ref, owner_ref, length_ref, places_ref, queries_ref, *refs):
     outs, rows = refs[:-1], refs[-1]
+    seq_count, most_pages = owner_ref.shape
     heads = queries_ref.shape[1] // HEAD_DIM
     spread_rows(queries_ref, rows)
-    plan = slot_plan(owner_ref, length_ref, places_ref, count, capacity)
+    gap = owner_ref[...] - lax.axis_index("store")
+    gap = jnp.where(gap < 0, gap + count, gap)
+    square = (seq_count, seq_count)
+    lengths = jnp.where(
+        lax.broadcasted_iota(jnp.int32, square, 0) == lax.broadcasted_iota(jnp.int32, square, 1),
+        length_ref[...].reshape(1, seq_count).astype(jnp.float32),
+        0.0,
+    )
+    lengths = jnp.sum(lengths, axis=1, keepdims=True)
+    page = lax.broadcasted_iota(jnp.int32, gap.shape, 1)
+    entry = lax.broadcasted_iota(jnp.int32, gap.shape, 0) * most_pages + page
+    gap = jnp.where(page.astype(jnp.float32) < lengths, gap, -1)
+    keys = (entry * FIELD + places_ref[...]).astype(jnp.float32)
+    span = float(most_pages * FIELD)
+    none = float(seq_count * most_pages * FIELD)
     line = lax.broadcasted_iota(jnp.int32, (PACKED_TILE, HEAD_DIM), 0)
     for step in range(1, REACH):
         out_ref = outs[step - 1]
-        note = jnp.zeros((PACKED_TILE, HEAD_DIM), jnp.int32)
+        left = jnp.where(gap == step, keys, none)
+        note = jnp.zeros((PACKED_TILE, HEAD_DIM), jnp.float32)
         for slot in range(capacity):
-            seq, place, _ = plan[step][slot]
-            out_ref[slot * heads : (slot + 1) * heads, :] = slot_rows(rows, seq, heads).astype(jnp.bfloat16)
+            key = jnp.min(jnp.min(left, axis=1, keepdims=True), axis=0, keepdims=True)
+            left = jnp.where(left > key, left, none)
+            value = rows[0:heads, :]
+            for seq in range(1, seq_count):
+                here = (key >= seq * span) & (key < (seq + 1) * span)
+                value = jnp.where(here, rows[seq * heads : (seq + 1) * heads, :], value)
+            out_ref[slot * heads : (slot + 1) * heads, :] = value.astype(jnp.bfloat16)
+            place = key - jnp.floor(key * (1.0 / FIELD)) * FIELD
             note = jnp.where(line == slot, place, note)
-        out_ref[capacity * heads :, :] = note.astype(jnp.float32).astype(jnp.bfloat16)
+        out_ref[capacity * heads :, :] = note.astype(jnp.bfloat16)
 
 
 def page_parts(slots, pages_ref, scale):
@@ -141,11 +163,17 @@
         (payload_ref[slot * heads : (slot + 1) * heads, :], notes[slot, 0].astype(jnp.int32))
         for slot in range(capacity)
     ]
-    marks = jnp.zeros((heads, HEAD_DIM), jnp.float32)
-    for slot, (peak, total, summed) in enumerate(page_parts(slots, pages_ref, scale)):
-        out_ref[slot * heads : (slot + 1) * heads, :] = summed
-        marks = marks + to_lanes(peak, slot * heads) + to_lanes(total, (capacity + slot) * heads)
+    parts = page_parts(slots, pages_ref, scale)
+    columns = [part[0] for part in parts] + [part[1] for part in parts]
+    lane = lax.broadcasted_iota(jnp.int32, (heads, HEAD_DIM), 1)
+    marks = columns[0]
+    for at in range(1, 2 * capacity):
+        marks = jnp.where(lane >= at * heads, columns[at], marks)
+    head = lax.broadcasted_iota(jnp.int32, (heads, HEAD_DIM), 0)
+    marks = jnp.where(lax.rem(lane, heads) == head, marks, 0.0)
     row = jnp.sum(marks, axis=0, keepdims=True)
+    for slot, part in enumerate(parts):
+        out_ref[slot * heads : (slot + 1) * heads, :] = part[2]
     out_ref[capacity * heads :, :] = jnp.broadcast_to(row, (TILE, HEAD_DIM))
 
 
@@ -231,7 +259,6 @@
     factors = [jnp.exp(peak - highest) for peak in peaks]
     share = functools.reduce(jnp.add, [factor * total for factor, total in zip(factors, totals)])
     inverse = 1.0 / over_slots(share, jnp.add)
-    factors = [factor * inverse for factor in factors]
     for seq in range(seq_count):
         line = slice(seq, seq + 1)
         numerator = to_column(factors[0][line], 0, heads) * state_ref[seq * heads : (seq + 1) * heads, :]
@@ -239,7 +266,7 @@
             for slot in range(capacity):
                 column = to_column(factor[line], slot * heads, heads)
                 numerator = numerator + column * part[slot * heads : (slot + 1) * heads, :]
-        rows[seq * heads : (seq + 1) * heads, :] = numerator
+        rows[seq * heads : (seq + 1) * heads, :] = numerator * to_column(inverse[line], 0, heads)
     for head in range(heads):
         out_ref[:, head * HEAD_DIM : (head + 1) * HEAD_DIM] = rows[
             pl.ds(head, seq_count, stride=heads), :
@@ -269,7 +296,7 @@
     payloads = pl.pallas_call(
         functools.partial(pack_kernel, count, capacity),
         out_shape=[sent] * (REACH - 1),
-        in_specs=[VMEM] + [SMEM] * 3 + [VMEM],
+        in_specs=[VMEM] * 5,
         out_specs=[VMEM] * (REACH - 1),
         scratch_shapes=scratch,
         compiler_params=PARAMS,

time: 19.3 us -> 18.8 us (0.974)
  Pallas kernels: 4.16 us -> 3.71 us
    pallas_call x1, Pallas kernels: 0.69 us -> 0.26 us  [body(): pl.pallas_call(functools.partial(pack_kernel, count, capacity), out_shape...]
  transfers between devices with their start and end apart: 6 -> 6, of which waited for: 3 -> 3; matrix products, arithmetic and copies ran while one was open for 0% -> 0% of each run, Pallas kernels for 13% -> 14%
where the time goes in v3:
time: 18.8 us; the launch traced here: 18.7 us
  starting transfers between devices  10.2 us (54%)
  waiting for transfers between devices  3.97 us (21%)
  Pallas kernels  3.71 us (20%)
  local copies, waits for them, and re-layouts  0.75 us (4%)
    ppermute x6, starting transfers between devices, shifted(): return lax.ppermute(value, axis, pairs)  10.2 us
    ppermute x6, waiting for transfers between devices, shifted(): return lax.ppermute(value, axis, pairs)  3.97 us
    pallas_call x3, Pallas kernels, body(): part = attend(payload, kv_pages)  1.46 us
    pallas_call x1, Pallas kernels, body(): pl.pallas_call(functools.partial(local_kernel, count, capacity, scale), o...  1.07 us
    pallas_call x1, Pallas kernels, body(): pl.pallas_call(functools.partial(combine_kernel, seq_count, capacity), ou...  0.92 us
    unnamed x12, local copies, waits for them, and re-layouts  0.75 us
  transfers between devices with their start and end apart: 6, of which 3 were waited for; matrix products, arithmetic and copies ran while one was open for 0% of the time, Pallas kernels for 14%

profile of v3, /device:TPU:0, one launch (start us, length us, event | category | flops | bytes accessed | tf_op | source)
XLA Modules:
  0.0 18.7 jit_solution(895813447308504896)
XLA Ops:
  0.0 0.0 copy-start.3
  0.0 0.0 copy-start.5
  0.0 0.0 copy-start.1
  0.0 0.0 copy-start.4
  0.0 0.7 %copy-done.3 = s32[2,4]{1,0:T(2,128)S(1)} copy-done((s32[2,4]{1,0:T(2,128)S(1)}, s32[2,4]{1,0:T(2,128)}, u32[]{:S(2)}) %copy-start.3) | copy-done | bytes 56
  0.7 0.0 copy-done.5
  0.7 0.1 copy-done.1
  0.8 0.0 copy-done.4
  0.8 0.0 copy-start
  0.8 0.3 %pack.1 = (bf16[80,128]{1,0:T(8,128)(2,1)S(1)}, bf16[80,128]{1,0:T(8,128)(2,1)S(1)}, bf16[80,128]{1,0:T(8,128)(2,1)S(1)}) custom-call(f32[8,128]{1,0:T(8,128)S(1)} %first.1.first_ref, s32[2,4]{1,0:T(2,128)S(1)} %copy-done.3, s32[2]{0:T(128)S(1)} %copy-done.5, s32[2,4]{1,0:T(2,128)S(1)} %copy-done.4, bf16[2,4096]{1,0:T(2,128)(2,1)S(1)} %copy-done.1), custom_call_target="tpu_custom_call" | custom-call | flops 999999995904 | tf_op jit(solution)/shard_map/pack/pallas_call | solution.py:296
  1.0 3.0 %collective-permute-start = (bf16[80,128]{1,0:T(8,128)(2,1)S(1)}, bf16[80,128]{1,0:T(8,128)(2,1)S(1)}, u32[]{:S(2)}, u32[]{:S(2)}) collective-permute-start(bf16[80,128]{1,0:T(8,128)(2,1)S(1)} %get-tuple-element.12), channel_id=1, source_target_pairs={{0,2},{2,4},{4,6},{6,8},{8,10},{10,12},{12,14},{14,0},{1,3},{3,5},... | collective-permute-start | bytes 61448 | tf_op jit(solution)/shard_map/ppermute | solution.py:24
  4.0 1.6 %collective-permute-start.2 = (bf16[80,128]{1,0:T(8,128)(2,1)S(1)}, bf16[80,128]{1,0:T(8,128)(2,1)S(1)}, u32[]{:S(2)}, u32[]{:S(2)}) collective-permute-start(bf16[80,128]{1,0:T(8,128)(2,1)S(1)} %get-tuple-element.13), channel_id=1, source_target_pairs={{0,4},{2,6},{4,8},{6,10},{8,12},{10,14},{12,0},{14,2},{1,5},{3,7},... | collective-permute-start | bytes 61448 | tf_op jit(solution)/shard_map/ppermute | solution.py:24
  5.6 2.6 %collective-permute-start.4 = (bf16[80,128]{1,0:T(8,128)(2,1)S(1)}, bf16[80,128]{1,0:T(8,128)(2,1)S(1)}, u32[]{:S(2)}, u32[]{:S(2)}) collective-permute-start(bf16[80,128]{1,0:T(8,128)(2,1)S(1)} %get-tuple-element.14), channel_id=1, source_target_pairs={{0,6},{2,8},{4,10},{6,12},{8,14},{10,0},{12,2},{14,4},{1,7},{3,9},... | collective-permute-start | bytes 61448 | tf_op jit(solution)/shard_map/ppermute | solution.py:24
  8.2 0.7 %collective-permute-done.payload_ref = bf16[80,128]{1,0:T(8,128)(2,1)S(1)} collective-permute-done((bf16[80,128]{1,0:T(8,128)(2,1)S(1)}, bf16[80,128]{1,0:T(8,128)(2,1)S(1)}, u32[]{:S(2)}, u32[]{:S(2)}) %collective-permute-start) | collective-permute-done | bytes 20512 | tf_op jit(solution)/shard_map/ppermute | solution.py:24
  8.8 0.0 copy-done
  8.8 0.5 %attend.3 = f32[72,128]{1,0:T(8,128)S(1)} custom-call(bf16[80,128]{1,0:T(8,128)(2,1)S(1)} %collective-permute-done.payload_ref, bf16[8,2,256,512]{3,2,1,0:T(8,128)(2,1)S(1)} %copy-done), custom_call_target="tpu_custom_call" | custom-call | tf_op jit(solution)/shard_map/attend/pallas_call | solution.py:317
  9.3 0.0 copy-start.2
  9.3 2.1 %collective-permute-start.1 = (f32[72,128]{1,0:T(8,128)S(1)}, f32[72,128]{1,0:T(8,128)S(1)}, u32[]{:S(2)}, u32[]{:S(2)}) collective-permute-start(f32[72,128]{1,0:T(8,128)S(1)} %attend.3), channel_id=1, source_target_pairs={{0,14},{2,0},{4,2},{6,4},{8,6},{10,8},{12,10},{14,12},{1,15},{3,1}... | collective-permute-start | bytes 110600 | tf_op jit(solution)/shard_map/ppermute | solution.py:24
  11.4 0.0 collective-permute-done.2.payload_ref
  11.4 0.5 %attend.4 = f32[72,128]{1,0:T(8,128)S(1)} custom-call(bf16[80,128]{1,0:T(8,128)(2,1)S(1)} %collective-permute-done.2.payload_ref, bf16[8,2,256,512]{3,2,1,0:T(8,128)(2,1)S(1)} %copy-done), custom_call_target="tpu_custom_call" | custom-call | tf_op jit(solution)/shard_map/attend/pallas_call | solution.py:317
  11.9 0.5 %collective-permute-start.3 = (f32[72,128]{1,0:T(8,128)S(1)}, f32[72,128]{1,0:T(8,128)S(1)}, u32[]{:S(2)}, u32[]{:S(2)}) collective-permute-start(f32[72,128]{1,0:T(8,128)S(1)} %attend.4), channel_id=1, source_target_pairs={{0,12},{2,14},{4,0},{6,2},{8,4},{10,6},{12,8},{14,10},{1,13},{3,15... | collective-permute-start | bytes 110600 | tf_op jit(solution)/shard_map/ppermute | solution.py:24
  12.4 0.0 collective-permute-done.4.payload_ref
  12.4 0.5 %attend.5 = f32[72,128]{1,0:T(8,128)S(1)} custom-call(bf16[80,128]{1,0:T(8,128)(2,1)S(1)} %collective-permute-done.4.payload_ref, bf16[8,2,256,512]{3,2,1,0:T(8,128)(2,1)S(1)} %copy-done), custom_call_target="tpu_custom_call" | custom-call | tf_op jit(solution)/shard_map/attend/pallas_call | solution.py:317
  12.9 0.5 %collective-permute-start.5 = (f32[72,128]{1,0:T(8,128)S(1)}, f32[72,128]{1,0:T(8,128)S(1)}, u32[]{:S(2)}, u32[]{:S(2)}) collective-permute-start(f32[72,128]{1,0:T(8,128)S(1)} %attend.5), channel_id=1, source_target_pairs={{0,10},{2,12},{4,14},{6,0},{8,2},{10,4},{12,6},{14,8},{1,11},{3,13... | collective-permute-start | bytes 110600 | tf_op jit(solution)/shard_map/ppermute | solution.py:24
  13.4 0.0 copy-done.2
  13.4 1.1 %local.1 = (f32[64,128]{1,0:T(8,128)S(1)}, f32[40,128]{1,0:T(8,128)S(1)}) custom-call(s32[2,4]{1,0:T(2,128)S(1)} %copy-done.3, s32[2]{0:T(128)S(1)} %copy-done.5, s32[2,4]{1,0:T(2,128)S(1)} %copy-done.4, bf16[2,4096]{1,0:T(2,128)(2,1)S(1)} %copy-done.1, bf16[2,2,512]{2,1,0:T(2,128)(2,1)S(1)} %copy-done.2, bf16[8,2,256,512]{3,2,1,0:T(8,128)(2,1)S(1)} %copy-done), custom_call_target="tpu_custom_call" | custom-call | tf_op jit(solution)/shard_map/local/pallas_call | solution.py:319
  14.4 0.0 collective-permute-done.1.refs_0_
  14.4 1.6 %collective-permute-done.3.refs_1_ = f32[72,128]{1,0:T(8,128)S(1)} collective-permute-done((f32[72,128]{1,0:T(8,128)S(1)}, f32[72,128]{1,0:T(8,128)S(1)}, u32[]{:S(2)}, u32[]{:S(2)}) %collective-permute-start.3) | collective-permute-done | bytes 36896 | tf_op jit(solution)/shard_map/ppermute | solution.py:24
  16.0 1.7 %collective-permute-done.5.refs_2_ = f32[72,128]{1,0:T(8,128)S(1)} collective-permute-done((f32[72,128]{1,0:T(8,128)S(1)}, f32[72,128]{1,0:T(8,128)S(1)}, u32[]{:S(2)}, u32[]{:S(2)}) %collective-permute-start.5) | collective-permute-done | bytes 36896 | tf_op jit(solution)/shard_map/ppermute | solution.py:24
  17.8 0.9 %combine.1 = bf16[2,4096]{1,0:T(2,128)(2,1)} custom-call(f32[64,128]{1,0:T(8,128)S(1)} %get-tuple-element.10.state_ref, f32[40,128]{1,0:T(8,128)S(1)} %get-tuple-element.11.bias_ref, f32[72,128]{1,0:T(8,128)S(1)} %collective-permute-done.1.refs_0_, f32[72,128]{1,0:T(8,128)S(1)} %collective-permute-done.3.refs_1_, f32[72,128]{1,0:T(8,128)S(1)} %collective-permute-done.5.refs_2_), custom_call_target="tpu_custom_call" | custom-call | tf_op jit(solution)/shard_map/combine/pallas_call | solution.py:331
  (1 shorter events, 0.0 us)
Async XLA Ops:
  0.0 0.7 %copy-start.3 = (s32[2,4]{1,0:T(2,128)S(1)}, s32[2,4]{1,0:T(2,128)}, u32[]{:S(2)}) copy-start(s32[2,4]{1,0:T(2,128)} %owner_ref.3) | copy-start | bytes 100
  0.0 0.7 %copy-start.5 = (s32[2]{0:T(128)S(1)}, s32[2]{0:T(128)}, u32[]{:S(2)}) copy-start(s32[2]{0:T(128)} %length_ref.3) | copy-start | bytes 28
  0.0 0.7 %copy-start.1 = (bf16[2,4096]{1,0:T(2,128)(2,1)S(1)}, bf16[2,4096]{1,0:T(2,128)(2,1)}, u32[]{:S(2)}) copy-start(bf16[2,4096]{1,0:T(2,128)(2,1)} %queries_ref.3) | copy-start | bytes 49156
  0.0 0.7 %copy-start.4 = (s32[2,4]{1,0:T(2,128)S(1)}, s32[2,4]{1,0:T(2,128)}, u32[]{:S(2)}) copy-start(s32[2,4]{1,0:T(2,128)} %places_ref.3) | copy-start | bytes 100
  0.8 8.1 %copy-start = (bf16[8,2,256,512]{3,2,1,0:T(8,128)(2,1)S(1)}, bf16[8,2,256,512]{3,2,1,0:T(8,128)(2,1)}, u32[]{:S(2)}) copy-start(bf16[8,2,256,512]{3,2,1,0:T(8,128)(2,1)} %pages_ref.7) | copy-start | bytes 12582916
  1.0 7.8 %collective-permute-start = (bf16[80,128]{1,0:T(8,128)(2,1)S(1)}, bf16[80,128]{1,0:T(8,128)(2,1)S(1)}, u32[]{:S(2)}, u32[]{:S(2)}) collective-permute-start(bf16[80,128]{1,0:T(8,128)(2,1)S(1)} %get-tuple-element.12), channel_id=1, source_target_pairs={{0,2},{2,4},{4,6},{6,8},{8,10},{10,12},{12,14},{14,0},{1,3},{3,5},... | collective-permute-start | bytes 61448 | tf_op jit(solution)/shard_map/ppermute | solution.py:24
  4.0 7.4 %collective-permute-start.2 = (bf16[80,128]{1,0:T(8,128)(2,1)S(1)}, bf16[80,128]{1,0:T(8,128)(2,1)S(1)}, u32[]{:S(2)}, u32[]{:S(2)}) collective-permute-start(bf16[80,128]{1,0:T(8,128)(2,1)S(1)} %get-tuple-element.13), channel_id=1, source_target_pairs={{0,4},{2,6},{4,8},{6,10},{8,12},{10,14},{12,0},{14,2},{1,5},{3,7},... | collective-permute-start | bytes 61448 | tf_op jit(solution)/shard_map/ppermute | solution.py:24
  5.6 6.8 %collective-permute-start.4 = (bf16[80,128]{1,0:T(8,128)(2,1)S(1)}, bf16[80,128]{1,0:T(8,128)(2,1)S(1)}, u32[]{:S(2)}, u32[]{:S(2)}) collective-permute-start(bf16[80,128]{1,0:T(8,128)(2,1)S(1)} %get-tuple-element.14), channel_id=1, source_target_pairs={{0,6},{2,8},{4,10},{6,12},{8,14},{10,0},{12,2},{14,4},{1,7},{3,9},... | collective-permute-start | bytes 61448 | tf_op jit(solution)/shard_map/ppermute | solution.py:24
  9.3 4.0 %copy-start.2 = (bf16[2,2,512]{2,1,0:T(2,128)(2,1)S(1)}, bf16[2,2,512]{2,1,0:T(2,128)(2,1)}, u32[]{:S(2)}) copy-start(bf16[2,2,512]{2,1,0:T(2,128)(2,1)} %fresh_ref.1) | copy-start | bytes 12292
  9.3 5.1 %collective-permute-start.1 = (f32[72,128]{1,0:T(8,128)S(1)}, f32[72,128]{1,0:T(8,128)S(1)}, u32[]{:S(2)}, u32[]{:S(2)}) collective-permute-start(f32[72,128]{1,0:T(8,128)S(1)} %attend.3), channel_id=1, source_target_pairs={{0,14},{2,0},{4,2},{6,4},{8,6},{10,8},{12,10},{14,12},{1,15},{3,1}... | collective-permute-start | bytes 110600 | tf_op jit(solution)/shard_map/ppermute | solution.py:24
  11.9 4.1 %collective-permute-start.3 = (f32[72,128]{1,0:T(8,128)S(1)}, f32[72,128]{1,0:T(8,128)S(1)}, u32[]{:S(2)}, u32[]{:S(2)}) collective-permute-start(f32[72,128]{1,0:T(8,128)S(1)} %attend.4), channel_id=1, source_target_pairs={{0,12},{2,14},{4,0},{6,2},{8,4},{10,6},{12,8},{14,10},{1,13},{3,15... | collective-permute-start | bytes 110600 | tf_op jit(solution)/shard_map/ppermute | solution.py:24
  12.9 4.9 %collective-permute-start.5 = (f32[72,128]{1,0:T(8,128)S(1)}, f32[72,128]{1,0:T(8,128)S(1)}, u32[]{:S(2)}, u32[]{:S(2)}) collective-permute-start(f32[72,128]{1,0:T(8,128)S(1)} %attend.5), channel_id=1, source_target_pairs={{0,10},{2,12},{4,14},{6,0},{8,2},{10,4},{12,6},{14,8},{1,11},{3,13... | collective-permute-start | bytes 110600 | tf_op jit(solution)/shard_map/ppermute | solution.py:24

commit v4 on v3

--- a/solution.py
+++ b/solution.py
@@ -16,6 +16,7 @@
 VMEM = pl.BlockSpec(memory_space=pltpu.VMEM)
 SMEM = pl.BlockSpec(memory_space=pltpu.SMEM)
 PARAMS = pltpu.CompilerParams(vmem_limit_bytes=16 * 2**20)
+BACKS = (1, 3, 2)
 
 
 def shifted(value, axis, steps):
@@ -179,7 +180,7 @@
 
 def local_kernel(
     count, capacity, scale, owner_ref, length_ref, places_ref, queries_ref, fresh_ref, pages_ref,
-    state_ref, bias_ref, rows
+    part_ref, state_ref, bias_ref, rows
 ):
     seq_count = queries_ref.shape[0]
     heads = queries_ref.shape[1] // HEAD_DIM
@@ -192,6 +193,16 @@
         pages_ref,
         scale,
     )
+    marks = part_ref[capacity * heads : capacity * heads + 1, :]
+    local += [
+        (
+            to_column(marks, slot * heads, heads),
+            to_column(marks, (capacity + slot) * heads, heads),
+            part_ref[slot * heads : (slot + 1) * heads, :],
+        )
+        for slot in range(capacity)
+    ]
+    held = plan[0] + plan[BACKS[0]]
     line = lax.broadcasted_iota(jnp.int32, (TILE, HEAD_DIM), 0)
     lane = lax.broadcasted_iota(jnp.int32, (TILE, HEAD_DIM), 1)
     peaks = jnp.full((TILE, HEAD_DIM), NEVER, jnp.float32)
@@ -211,12 +222,12 @@
 
         own = jnp.sum(query * fresh(0), axis=1, keepdims=True) * scale
         highest = own
-        for (at, _, used), (peak, _, _) in zip(plan[0], local):
+        for (at, _, used), (peak, _, _) in zip(held, local):
             highest = jnp.maximum(highest, jnp.where((used > 0) & (at == seq), peak, NEVER))
         own_weight = jnp.exp(own - highest)
         denominator = own_weight
         numerator = own_weight * fresh(1)
-        for (at, _, used), (peak, total, summed) in zip(plan[0], local):
+        for (at, _, used), (peak, total, summed) in zip(held, local):
             inside = (used > 0) & (at == seq)
             factor = jnp.exp(jnp.where(inside, peak - highest, NEVER))
             denominator = denominator + factor * total
@@ -227,14 +238,14 @@
         peaks = jnp.where((line == seq) & (lane < heads), high_row, peaks)
         totals = jnp.where(line == seq, total_row, totals)
     bias_ref[0:TILE, :] = peaks
-    for step in range(1, REACH):
+    for tile, step in enumerate(BACKS[1:], 1):
         bias = jnp.full((TILE, HEAD_DIM), NEVER, jnp.float32)
         for slot in range(capacity):
             at, _, used = plan[step][slot]
             mine = (line == at) & (lane // heads == slot) & (used > 0)
             bias = jnp.where(mine, 0.0, bias)
-        bias_ref[step * TILE : (step + 1) * TILE, :] = bias
-    bias_ref[REACH * TILE :, :] = totals
+        bias_ref[tile * TILE : (tile + 1) * TILE, :] = bias
+    bias_ref[(REACH - 1) * TILE :, :] = totals
 
 
 def combine_kernel(seq_count, capacity, state_ref, bias_ref, *refs):
@@ -244,7 +255,7 @@
     peaks = [bias_ref[0:TILE, :]] + [
         mark + bias_ref[(at + 1) * TILE : (at + 2) * TILE, :] for at, mark in enumerate(marks)
     ]
-    totals = [bias_ref[REACH * TILE :, :]] + [
+    totals = [bias_ref[(REACH - 1) * TILE :, :]] + [
         pltpu.roll(mark, HEAD_DIM - capacity * heads, 1) for mark in marks
     ]
 
@@ -259,6 +270,7 @@
     factors = [jnp.exp(peak - highest) for peak in peaks]
     share = functools.reduce(jnp.add, [factor * total for factor, total in zip(factors, totals)])
     inverse = 1.0 / over_slots(share, jnp.add)
+    factors = [factor * inverse for factor in factors]
     for seq in range(seq_count):
         line = slice(seq, seq + 1)
         numerator = to_column(factors[0][line], 0, heads) * state_ref[seq * heads : (seq + 1) * heads, :]
@@ -266,7 +278,7 @@
             for slot in range(capacity):
                 column = to_column(factor[line], slot * heads, heads)
                 numerator = numerator + column * part[slot * heads : (slot + 1) * heads, :]
-        rows[seq * heads : (seq + 1) * heads, :] = numerator * to_column(inverse[line], 0, heads)
+        rows[seq * heads : (seq + 1) * heads, :] = numerator
     for head in range(heads):
         out_ref[:, head * HEAD_DIM : (head + 1) * HEAD_DIM] = rows[
             pl.ds(head, seq_count, stride=heads), :
@@ -311,32 +323,32 @@
         compiler_params=PARAMS,
         name="attend",
     )
-    parts = []
+    parts = {}
     for step in range(1, REACH):
         payload = shifted(payloads[step - 1], "store", step)
         part = attend(payload, kv_pages)
-        parts.append(shifted(part, "store", -step))
+        parts[step] = shifted(part, "store", -step)
     state, bias = pl.pallas_call(
         functools.partial(local_kernel, count, capacity, scale),
         out_shape=[
             jax.ShapeDtypeStruct((seq_count * heads, HEAD_DIM), jnp.float32),
-            jax.ShapeDtypeStruct(((REACH + 1) * TILE, HEAD_DIM), jnp.float32),
+            jax.ShapeDtypeStruct((REACH * TILE, HEAD_DIM), jnp.float32),
         ],
-        in_specs=[SMEM] * 3 + [VMEM] * 3,
+        in_specs=[SMEM] * 3 + [VMEM] * 4,
         out_specs=[VMEM] * 2,
         scratch_shapes=scratch,
         compiler_params=PARAMS,
         name="local",
-    )(page_owner, seq_pages, page_index, queries, new_kv, kv_pages)
+    )(page_owner, seq_pages, page_index, queries, new_kv, kv_pages, parts[BACKS[0]])
     return pl.pallas_call(
         functools.partial(combine_kernel, seq_count, capacity),
         out_shape=jax.ShapeDtypeStruct(queries.shape, queries.dtype),
-        in_specs=[VMEM] * (1 + REACH),
+        in_specs=[VMEM] * REACH,
         out_specs=VMEM,
         scratch_shapes=scratch,
         compiler_params=PARAMS,
         name="combine",
-    )(state, bias, *parts)
+    )(state, bias, *[parts[step] for step in BACKS[1:]])
 
 
 def solution(mesh):

time: 18.8 us -> 18.9 us (level)
  no operation moved by 1% of the time
where the time goes in v4:
time: 18.9 us; the launch traced here: 18.7 us
  starting transfers between devices  10.2 us (54%)
  waiting for transfers between devices  3.97 us (21%)
  Pallas kernels  3.71 us (20%)
  local copies, waits for them, and re-layouts  0.76 us (4%)
    ppermute x6, starting transfers between devices, shifted(): return lax.ppermute(value, axis, pairs)  10.2 us
    ppermute x6, waiting for transfers between devices, shifted(): return lax.ppermute(value, axis, pairs)  3.97 us
    pallas_call x3, Pallas kernels, body(): part = attend(payload, kv_pages)  1.46 us
    pallas_call x1, Pallas kernels, body(): pl.pallas_call(functools.partial(local_kernel, count, capacity, scale), o...  1.08 us
    pallas_call x1, Pallas kernels, body(): pl.pallas_call(functools.partial(combine_kernel, seq_count, capacity), ou...  0.91 us
    unnamed x12, local copies, waits for them, and re-layouts  0.76 us
  transfers between devices with their start and end apart: 6, of which 3 were waited for; matrix products, arithmetic and copies ran while one was open for 0% of the time, Pallas kernels for 14%

profile of v4, /device:TPU:0, one launch (start us, length us, event | category | flops | bytes accessed | tf_op | source)
XLA Modules:
  0.0 18.7 jit_solution(18347705507458983393)
XLA Ops:
  0.0 0.0 copy-start.5
  0.0 0.0 copy-start.3
  0.0 0.0 copy-start.4
  0.0 0.0 copy-start.1
  0.0 0.6 %copy-done.5 = s32[2]{0:T(128)S(1)} copy-done((s32[2]{0:T(128)S(1)}, s32[2]{0:T(128)}, u32[]{:S(2)}) %copy-start.5) | copy-done | bytes 32
  0.7 0.0 copy-done.3
  0.7 0.0 copy-done.4
  0.7 0.1 copy-done.1
  0.8 0.0 copy-start
  0.8 0.3 %pack.1 = (bf16[80,128]{1,0:T(8,128)(2,1)S(1)}, bf16[80,128]{1,0:T(8,128)(2,1)S(1)}, bf16[80,128]{1,0:T(8,128)(2,1)S(1)}) custom-call(f32[8,128]{1,0:T(8,128)S(1)} %first.1.first_ref, s32[2,4]{1,0:T(2,128)S(1)} %copy-done.3, s32[2]{0:T(128)S(1)} %copy-done.5, s32[2,4]{1,0:T(2,128)S(1)} %copy-done.4, bf16[2,4096]{1,0:T(2,128)(2,1)S(1)} %copy-done.1), custom_call_target="tpu_custom_call" | custom-call | flops 999999995904 | tf_op jit(solution)/shard_map/pack/pallas_call | solution.py:308
  1.0 3.0 %collective-permute-start = (bf16[80,128]{1,0:T(8,128)(2,1)S(1)}, bf16[80,128]{1,0:T(8,128)(2,1)S(1)}, u32[]{:S(2)}, u32[]{:S(2)}) collective-permute-start(bf16[80,128]{1,0:T(8,128)(2,1)S(1)} %get-tuple-element.10), channel_id=1, source_target_pairs={{0,2},{2,4},{4,6},{6,8},{8,10},{10,12},{12,14},{14,0},{1,3},{3,5},... | collective-permute-start | bytes 61448 | tf_op jit(solution)/shard_map/ppermute | solution.py:25
  4.1 1.6 %collective-permute-start.4 = (bf16[80,128]{1,0:T(8,128)(2,1)S(1)}, bf16[80,128]{1,0:T(8,128)(2,1)S(1)}, u32[]{:S(2)}, u32[]{:S(2)}) collective-permute-start(bf16[80,128]{1,0:T(8,128)(2,1)S(1)} %get-tuple-element.14), channel_id=1, source_target_pairs={{0,4},{2,6},{4,8},{6,10},{8,12},{10,14},{12,0},{14,2},{1,5},{3,7},... | collective-permute-start | bytes 61448 | tf_op jit(solution)/shard_map/ppermute | solution.py:25
  5.6 2.6 %collective-permute-start.2 = (bf16[80,128]{1,0:T(8,128)(2,1)S(1)}, bf16[80,128]{1,0:T(8,128)(2,1)S(1)}, u32[]{:S(2)}, u32[]{:S(2)}) collective-permute-start(bf16[80,128]{1,0:T(8,128)(2,1)S(1)} %get-tuple-element.13), channel_id=1, source_target_pairs={{0,6},{2,8},{4,10},{6,12},{8,14},{10,0},{12,2},{14,4},{1,7},{3,9},... | collective-permute-start | bytes 61448 | tf_op jit(solution)/shard_map/ppermute | solution.py:25
  8.2 0.7 %collective-permute-done.payload_ref = bf16[80,128]{1,0:T(8,128)(2,1)S(1)} collective-permute-done((bf16[80,128]{1,0:T(8,128)(2,1)S(1)}, bf16[80,128]{1,0:T(8,128)(2,1)S(1)}, u32[]{:S(2)}, u32[]{:S(2)}) %collective-permute-start) | collective-permute-done | bytes 20512 | tf_op jit(solution)/shard_map/ppermute | solution.py:25
  8.9 0.0 copy-done
  8.9 0.5 %attend.3 = f32[72,128]{1,0:T(8,128)S(1)} custom-call(bf16[80,128]{1,0:T(8,128)(2,1)S(1)} %collective-permute-done.payload_ref, bf16[8,2,256,512]{3,2,1,0:T(8,128)(2,1)S(1)} %copy-done), custom_call_target="tpu_custom_call" | custom-call | tf_op jit(solution)/shard_map/attend/pallas_call | solution.py:329
  9.3 0.0 copy-start.2
  9.3 2.1 %collective-permute-start.1 = (f32[72,128]{1,0:T(8,128)S(1)}, f32[72,128]{1,0:T(8,128)S(1)}, u32[]{:S(2)}, u32[]{:S(2)}) collective-permute-start(f32[72,128]{1,0:T(8,128)S(1)} %attend.3), channel_id=1, source_target_pairs={{0,14},{2,0},{4,2},{6,4},{8,6},{10,8},{12,10},{14,12},{1,15},{3,1}... | collective-permute-start | bytes 110600 | tf_op jit(solution)/shard_map/ppermute | solution.py:25
  11.4 0.0 collective-permute-done.4.payload_ref
  11.4 0.5 %attend.5 = f32[72,128]{1,0:T(8,128)S(1)} custom-call(bf16[80,128]{1,0:T(8,128)(2,1)S(1)} %collective-permute-done.4.payload_ref, bf16[8,2,256,512]{3,2,1,0:T(8,128)(2,1)S(1)} %copy-done), custom_call_target="tpu_custom_call" | custom-call | tf_op jit(solution)/shard_map/attend/pallas_call | solution.py:329
  11.9 0.5 %collective-permute-start.5 = (f32[72,128]{1,0:T(8,128)S(1)}, f32[72,128]{1,0:T(8,128)S(1)}, u32[]{:S(2)}, u32[]{:S(2)}) collective-permute-start(f32[72,128]{1,0:T(8,128)S(1)} %attend.5), channel_id=1, source_target_pairs={{0,12},{2,14},{4,0},{6,2},{8,4},{10,6},{12,8},{14,10},{1,13},{3,15... | collective-permute-start | bytes 110600 | tf_op jit(solution)/shard_map/ppermute | solution.py:25
  12.4 0.0 collective-permute-done.2.payload_ref
  12.4 0.5 %attend.4 = f32[72,128]{1,0:T(8,128)S(1)} custom-call(bf16[80,128]{1,0:T(8,128)(2,1)S(1)} %collective-permute-done.2.payload_ref, bf16[8,2,256,512]{3,2,1,0:T(8,128)(2,1)S(1)} %copy-done), custom_call_target="tpu_custom_call" | custom-call | tf_op jit(solution)/shard_map/attend/pallas_call | solution.py:329
  12.9 0.5 %collective-permute-start.3 = (f32[72,128]{1,0:T(8,128)S(1)}, f32[72,128]{1,0:T(8,128)S(1)}, u32[]{:S(2)}, u32[]{:S(2)}) collective-permute-start(f32[72,128]{1,0:T(8,128)S(1)} %attend.4), channel_id=1, source_target_pairs={{0,10},{2,12},{4,14},{6,0},{8,2},{10,4},{12,6},{14,8},{1,11},{3,13... | collective-permute-start | bytes 110600 | tf_op jit(solution)/shard_map/ppermute | solution.py:25
  13.4 0.0 collective-permute-done.1.part_ref
  13.4 0.0 copy-done.2
  13.4 1.1 %local.1 = (f32[64,128]{1,0:T(8,128)S(1)}, f32[32,128]{1,0:T(8,128)S(1)}) custom-call(s32[2,4]{1,0:T(2,128)S(1)} %copy-done.3, s32[2]{0:T(128)S(1)} %copy-done.5, s32[2,4]{1,0:T(2,128)S(1)} %copy-done.4, bf16[2,4096]{1,0:T(2,128)(2,1)S(1)} %copy-done.1, bf16[2,2,512]{2,1,0:T(2,128)(2,1)S(1)} %copy-done.2, bf16[8,2,256,512]{3,2,1,0:T(8,128)(2,1)S(1)} %copy-done, ...), custom_call_target="tpu_custom_call" | custom-call | tf_op jit(solution)/shard_map/local/pallas_call | solution.py:331
  14.5 1.6 %collective-permute-done.5.refs_1_ = f32[72,128]{1,0:T(8,128)S(1)} collective-permute-done((f32[72,128]{1,0:T(8,128)S(1)}, f32[72,128]{1,0:T(8,128)S(1)}, u32[]{:S(2)}, u32[]{:S(2)}) %collective-permute-start.5) | collective-permute-done | bytes 36896 | tf_op jit(solution)/shard_map/ppermute | solution.py:25
  16.0 1.7 %collective-permute-done.3.refs_0_ = f32[72,128]{1,0:T(8,128)S(1)} collective-permute-done((f32[72,128]{1,0:T(8,128)S(1)}, f32[72,128]{1,0:T(8,128)S(1)}, u32[]{:S(2)}, u32[]{:S(2)}) %collective-permute-start.3) | collective-permute-done | bytes 36896 | tf_op jit(solution)/shard_map/ppermute | solution.py:25
  17.8 0.9 %combine.1 = bf16[2,4096]{1,0:T(2,128)(2,1)} custom-call(f32[64,128]{1,0:T(8,128)S(1)} %get-tuple-element.11.state_ref, f32[32,128]{1,0:T(8,128)S(1)} %get-tuple-element.12.bias_ref, f32[72,128]{1,0:T(8,128)S(1)} %collective-permute-done.3.refs_0_, f32[72,128]{1,0:T(8,128)S(1)} %collective-permute-done.5.refs_1_), custom_call_target="tpu_custom_call" | custom-call | tf_op jit(solution)/shard_map/combine/pallas_call | solution.py:343
  (1 shorter events, 0.0 us)
Async XLA Ops:
  0.0 0.7 %copy-start.5 = (s32[2]{0:T(128)S(1)}, s32[2]{0:T(128)}, u32[]{:S(2)}) copy-start(s32[2]{0:T(128)} %length_ref.3) | copy-start | bytes 28
  0.0 0.7 %copy-start.3 = (s32[2,4]{1,0:T(2,128)S(1)}, s32[2,4]{1,0:T(2,128)}, u32[]{:S(2)}) copy-start(s32[2,4]{1,0:T(2,128)} %owner_ref.3) | copy-start | bytes 100
  0.0 0.7 %copy-start.4 = (s32[2,4]{1,0:T(2,128)S(1)}, s32[2,4]{1,0:T(2,128)}, u32[]{:S(2)}) copy-start(s32[2,4]{1,0:T(2,128)} %places_ref.3) | copy-start | bytes 100
  0.0 0.8 %copy-start.1 = (bf16[2,4096]{1,0:T(2,128)(2,1)S(1)}, bf16[2,4096]{1,0:T(2,128)(2,1)}, u32[]{:S(2)}) copy-start(bf16[2,4096]{1,0:T(2,128)(2,1)} %queries_ref.3) | copy-start | bytes 49156
  0.8 8.1 %copy-start = (bf16[8,2,256,512]{3,2,1,0:T(8,128)(2,1)S(1)}, bf16[8,2,256,512]{3,2,1,0:T(8,128)(2,1)}, u32[]{:S(2)}) copy-start(bf16[8,2,256,512]{3,2,1,0:T(8,128)(2,1)} %pages_ref.7) | copy-start | bytes 12582916
  1.0 7.8 %collective-permute-start = (bf16[80,128]{1,0:T(8,128)(2,1)S(1)}, bf16[80,128]{1,0:T(8,128)(2,1)S(1)}, u32[]{:S(2)}, u32[]{:S(2)}) collective-permute-start(bf16[80,128]{1,0:T(8,128)(2,1)S(1)} %get-tuple-element.10), channel_id=1, source_target_pairs={{0,2},{2,4},{4,6},{6,8},{8,10},{10,12},{12,14},{14,0},{1,3},{3,5},... | collective-permute-start | bytes 61448 | tf_op jit(solution)/shard_map/ppermute | solution.py:25
  4.1 7.4 %collective-permute-start.4 = (bf16[80,128]{1,0:T(8,128)(2,1)S(1)}, bf16[80,128]{1,0:T(8,128)(2,1)S(1)}, u32[]{:S(2)}, u32[]{:S(2)}) collective-permute-start(bf16[80,128]{1,0:T(8,128)(2,1)S(1)} %get-tuple-element.14), channel_id=1, source_target_pairs={{0,4},{2,6},{4,8},{6,10},{8,12},{10,14},{12,0},{14,2},{1,5},{3,7},... | collective-permute-start | bytes 61448 | tf_op jit(solution)/shard_map/ppermute | solution.py:25
  5.6 6.8 %collective-permute-start.2 = (bf16[80,128]{1,0:T(8,128)(2,1)S(1)}, bf16[80,128]{1,0:T(8,128)(2,1)S(1)}, u32[]{:S(2)}, u32[]{:S(2)}) collective-permute-start(bf16[80,128]{1,0:T(8,128)(2,1)S(1)} %get-tuple-element.13), channel_id=1, source_target_pairs={{0,6},{2,8},{4,10},{6,12},{8,14},{10,0},{12,2},{14,4},{1,7},{3,9},... | collective-permute-start | bytes 61448 | tf_op jit(solution)/shard_map/ppermute | solution.py:25
  9.3 4.0 %copy-start.2 = (bf16[2,2,512]{2,1,0:T(2,128)(2,1)S(1)}, bf16[2,2,512]{2,1,0:T(2,128)(2,1)}, u32[]{:S(2)}) copy-start(bf16[2,2,512]{2,1,0:T(2,128)(2,1)} %fresh_ref.1) | copy-start | bytes 12292
  9.3 4.0 %collective-permute-start.1 = (f32[72,128]{1,0:T(8,128)S(1)}, f32[72,128]{1,0:T(8,128)S(1)}, u32[]{:S(2)}, u32[]{:S(2)}) collective-permute-start(f32[72,128]{1,0:T(8,128)S(1)} %attend.3), channel_id=1, source_target_pairs={{0,14},{2,0},{4,2},{6,4},{8,6},{10,8},{12,10},{14,12},{1,15},{3,1}... | collective-permute-start | bytes 110600 | tf_op jit(solution)/shard_map/ppermute | solution.py:25
  11.9 4.1 %collective-permute-start.5 = (f32[72,128]{1,0:T(8,128)S(1)}, f32[72,128]{1,0:T(8,128)S(1)}, u32[]{:S(2)}, u32[]{:S(2)}) collective-permute-start(f32[72,128]{1,0:T(8,128)S(1)} %attend.5), channel_id=1, source_target_pairs={{0,12},{2,14},{4,0},{6,2},{8,4},{10,6},{12,8},{14,10},{1,13},{3,15... | collective-permute-start | bytes 110600 | tf_op jit(solution)/shard_map/ppermute | solution.py:25
  12.9 4.9 %collective-permute-start.3 = (f32[72,128]{1,0:T(8,128)S(1)}, f32[72,128]{1,0:T(8,128)S(1)}, u32[]{:S(2)}, u32[]{:S(2)}) collective-permute-start(f32[72,128]{1,0:T(8,128)S(1)} %attend.4), channel_id=1, source_target_pairs={{0,10},{2,12},{4,14},{6,0},{8,2},{10,4},{12,6},{14,8},{1,11},{3,13... | collective-permute-start | bytes 110600 | tf_op jit(solution)/shard_map/ppermute | solution.py:25

commit v5 on v3

--- a/solution.py
+++ b/solution.py
@@ -10,7 +10,7 @@
 HEAD_DIM = 128
 REACH = 4
 TILE = 8
-PACKED_TILE = 16
+PACKED_TILE = 8
 NEVER = -1e30
 FIELD = 256
 VMEM = pl.BlockSpec(memory_space=pltpu.VMEM)
@@ -163,17 +163,11 @@
         (payload_ref[slot * heads : (slot + 1) * heads, :], notes[slot, 0].astype(jnp.int32))
         for slot in range(capacity)
     ]
-    parts = page_parts(slots, pages_ref, scale)
-    columns = [part[0] for part in parts] + [part[1] for part in parts]
-    lane = lax.broadcasted_iota(jnp.int32, (heads, HEAD_DIM), 1)
-    marks = columns[0]
-    for at in range(1, 2 * capacity):
-        marks = jnp.where(lane >= at * heads, columns[at], marks)
-    head = lax.broadcasted_iota(jnp.int32, (heads, HEAD_DIM), 0)
-    marks = jnp.where(lax.rem(lane, heads) == head, marks, 0.0)
+    marks = jnp.zeros((heads, HEAD_DIM), jnp.float32)
+    for slot, (peak, total, summed) in enumerate(page_parts(slots, pages_ref, scale)):
+        out_ref[slot * heads : (slot + 1) * heads, :] = summed
+        marks = marks + to_lanes(peak, slot * heads) + to_lanes(total, (capacity + slot) * heads)
     row = jnp.sum(marks, axis=0, keepdims=True)
-    for slot, part in enumerate(parts):
-        out_ref[slot * heads : (slot + 1) * heads, :] = part[2]
     out_ref[capacity * heads :, :] = jnp.broadcast_to(row, (TILE, HEAD_DIM))
 
 
@@ -259,6 +253,7 @@
     factors = [jnp.exp(peak - highest) for peak in peaks]
     share = functools.reduce(jnp.add, [factor * total for factor, total in zip(factors, totals)])
     inverse = 1.0 / over_slots(share, jnp.add)
+    factors = [factor * inverse for factor in factors]
     for seq in range(seq_count):
         line = slice(seq, seq + 1)
         numerator = to_column(factors[0][line], 0, heads) * state_ref[seq * heads : (seq + 1) * heads, :]
@@ -266,7 +261,7 @@
             for slot in range(capacity):
                 column = to_column(factor[line], slot * heads, heads)
                 numerator = numerator + column * part[slot * heads : (slot + 1) * heads, :]
-        rows[seq * heads : (seq + 1) * heads, :] = numerator * to_column(inverse[line], 0, heads)
+        rows[seq * heads : (seq + 1) * heads, :] = numerator
     for head in range(heads):
         out_ref[:, head * HEAD_DIM : (head + 1) * HEAD_DIM] = rows[
             pl.ds(head, seq_count, stride=heads), :

time: 18.8 us -> 18.9 us (level)
  starting transfers between devices: 10.2 us -> 12.5 us
  waiting for transfers between devices: 3.97 us -> 1.7 us
    ppermute x6, waiting for transfers between devices: 3.97 us -> 1.7 us  [shifted(): return lax.ppermute(value, axis, pairs)]
    ppermute x6, starting transfers between devices: 10.2 us -> 12.5 us  [shifted(): return lax.ppermute(value, axis, pairs)]
  transfers between devices with their start and end apart: 6 -> 6, of which waited for: 3 -> 2; matrix products, arithmetic and copies ran while one was open for 0% -> 0% of each run, Pallas kernels for 14% -> 14%
where the time goes in v5:
time: 18.9 us; the launch traced here: 18.7 us
  starting transfers between devices  12.5 us (66%)
  Pallas kernels  3.73 us (20%)
  waiting for transfers between devices  1.7 us (9%)
  local copies, waits for them, and re-layouts  0.76 us (4%)
    ppermute x6, starting transfers between devices, shifted(): return lax.ppermute(value, axis, pairs)  12.5 us
    ppermute x6, waiting for transfers between devices, shifted(): return lax.ppermute(value, axis, pairs)  1.7 us
    pallas_call x3, Pallas kernels, body(): part = attend(payload, kv_pages)  1.47 us
    pallas_call x1, Pallas kernels, body(): pl.pallas_call(functools.partial(local_kernel, count, capacity, scale), o...  1.07 us
    pallas_call x1, Pallas kernels, body(): pl.pallas_call(functools.partial(combine_kernel, seq_count, capacity), ou...  0.93 us
    unnamed x12, local copies, waits for them, and re-layouts  0.76 us
  transfers between devices with their start and end apart: 6, of which 2 were waited for; matrix products, arithmetic and copies ran while one was open for 0% of the time, Pallas kernels for 14%

profile of v5, /device:TPU:0, one launch (start us, length us, event | category | flops | bytes accessed | tf_op | source)
XLA Modules:
  0.0 18.7 jit_solution(7435235928335862755)
XLA Ops:
  0.0 0.0 copy-start.5
  0.0 0.0 copy-start.3
  0.0 0.0 copy-start.4
  0.0 0.0 copy-start.1
  0.0 0.6 %copy-done.5 = s32[2]{0:T(128)S(1)} copy-done((s32[2]{0:T(128)S(1)}, s32[2]{0:T(128)}, u32[]{:S(2)}) %copy-start.5) | copy-done | bytes 32
  0.7 0.0 copy-done.3
  0.7 0.0 copy-done.4
  0.7 0.1 copy-done.1
  0.8 0.0 copy-start
  0.8 0.3 %pack.1 = (bf16[72,128]{1,0:T(8,128)(2,1)S(1)}, bf16[72,128]{1,0:T(8,128)(2,1)S(1)}, bf16[72,128]{1,0:T(8,128)(2,1)S(1)}) custom-call(f32[8,128]{1,0:T(8,128)S(1)} %first.1.first_ref, s32[2,4]{1,0:T(2,128)S(1)} %copy-done.3, s32[2]{0:T(128)S(1)} %copy-done.5, s32[2,4]{1,0:T(2,128)S(1)} %copy-done.4, bf16[2,4096]{1,0:T(2,128)(2,1)S(1)} %copy-done.1), custom_call_target="tpu_custom_call" | custom-call | flops 999999995904 | tf_op jit(solution)/shard_map/pack/pallas_call | solution.py:291
  1.0 4.0 %collective-permute-start.4 = (bf16[72,128]{1,0:T(8,128)(2,1)S(1)}, bf16[72,128]{1,0:T(8,128)(2,1)S(1)}, u32[]{:S(2)}, u32[]{:S(2)}) collective-permute-start(bf16[72,128]{1,0:T(8,128)(2,1)S(1)} %get-tuple-element.14), channel_id=1, source_target_pairs={{0,6},{2,8},{4,10},{6,12},{8,14},{10,0},{12,2},{14,4},{1,7},{3,9},... | collective-permute-start | bytes 55304 | tf_op jit(solution)/shard_map/ppermute | solution.py:24
  5.1 1.6 %collective-permute-start.2 = (bf16[72,128]{1,0:T(8,128)(2,1)S(1)}, bf16[72,128]{1,0:T(8,128)(2,1)S(1)}, u32[]{:S(2)}, u32[]{:S(2)}) collective-permute-start(bf16[72,128]{1,0:T(8,128)(2,1)S(1)} %get-tuple-element.13), channel_id=1, source_target_pairs={{0,4},{2,6},{4,8},{6,10},{8,12},{10,14},{12,0},{14,2},{1,5},{3,7},... | collective-permute-start | bytes 55304 | tf_op jit(solution)/shard_map/ppermute | solution.py:24
  6.6 1.5 %collective-permute-start = (bf16[72,128]{1,0:T(8,128)(2,1)S(1)}, bf16[72,128]{1,0:T(8,128)(2,1)S(1)}, u32[]{:S(2)}, u32[]{:S(2)}) collective-permute-start(bf16[72,128]{1,0:T(8,128)(2,1)S(1)} %get-tuple-element.12), channel_id=1, source_target_pairs={{0,2},{2,4},{4,6},{6,8},{8,10},{10,12},{12,14},{14,0},{1,3},{3,5},... | collective-permute-start | bytes 55304 | tf_op jit(solution)/shard_map/ppermute | solution.py:24
  8.2 0.0 collective-permute-done.4.payload_ref
  8.2 0.0 copy-done
  8.2 0.5 %attend.5 = f32[72,128]{1,0:T(8,128)S(1)} custom-call(bf16[72,128]{1,0:T(8,128)(2,1)S(1)} %collective-permute-done.4.payload_ref, bf16[8,2,256,512]{3,2,1,0:T(8,128)(2,1)S(1)} %copy-done), custom_call_target="tpu_custom_call" | custom-call | tf_op jit(solution)/shard_map/attend/pallas_call | solution.py:312
  8.7 0.0 copy-start.2
  8.7 2.6 %collective-permute-start.5 = (f32[72,128]{1,0:T(8,128)S(1)}, f32[72,128]{1,0:T(8,128)S(1)}, u32[]{:S(2)}, u32[]{:S(2)}) collective-permute-start(f32[72,128]{1,0:T(8,128)S(1)} %attend.5), channel_id=1, source_target_pairs={{0,10},{2,12},{4,14},{6,0},{8,2},{10,4},{12,6},{14,8},{1,11},{3,13... | collective-permute-start | bytes 110600 | tf_op jit(solution)/shard_map/ppermute | solution.py:24
  11.3 0.0 collective-permute-done.2.payload_ref
  11.3 0.5 %attend.4 = f32[72,128]{1,0:T(8,128)S(1)} custom-call(bf16[72,128]{1,0:T(8,128)(2,1)S(1)} %collective-permute-done.2.payload_ref, bf16[8,2,256,512]{3,2,1,0:T(8,128)(2,1)S(1)} %copy-done), custom_call_target="tpu_custom_call" | custom-call | tf_op jit(solution)/shard_map/attend/pallas_call | solution.py:312
  11.8 1.4 %collective-permute-start.3 = (f32[72,128]{1,0:T(8,128)S(1)}, f32[72,128]{1,0:T(8,128)S(1)}, u32[]{:S(2)}, u32[]{:S(2)}) collective-permute-start(f32[72,128]{1,0:T(8,128)S(1)} %attend.4), channel_id=1, source_target_pairs={{0,12},{2,14},{4,0},{6,2},{8,4},{10,6},{12,8},{14,10},{1,13},{3,15... | collective-permute-start | bytes 110600 | tf_op jit(solution)/shard_map/ppermute | solution.py:24
  13.2 0.1 collective-permute-done.payload_ref
  13.3 0.5 %attend.3 = f32[72,128]{1,0:T(8,128)S(1)} custom-call(bf16[72,128]{1,0:T(8,128)(2,1)S(1)} %collective-permute-done.payload_ref, bf16[8,2,256,512]{3,2,1,0:T(8,128)(2,1)S(1)} %copy-done), custom_call_target="tpu_custom_call" | custom-call | tf_op jit(solution)/shard_map/attend/pallas_call | solution.py:312
  13.8 1.3 %collective-permute-start.1 = (f32[72,128]{1,0:T(8,128)S(1)}, f32[72,128]{1,0:T(8,128)S(1)}, u32[]{:S(2)}, u32[]{:S(2)}) collective-permute-start(f32[72,128]{1,0:T(8,128)S(1)} %attend.3), channel_id=1, source_target_pairs={{0,14},{2,0},{4,2},{6,4},{8,6},{10,8},{12,10},{14,12},{1,15},{3,1}... | collective-permute-start | bytes 110600 | tf_op jit(solution)/shard_map/ppermute | solution.py:24
  15.1 0.0 copy-done.2
  15.1 1.1 %local.1 = (f32[64,128]{1,0:T(8,128)S(1)}, f32[40,128]{1,0:T(8,128)S(1)}) custom-call(s32[2,4]{1,0:T(2,128)S(1)} %copy-done.3, s32[2]{0:T(128)S(1)} %copy-done.5, s32[2,4]{1,0:T(2,128)S(1)} %copy-done.4, bf16[2,4096]{1,0:T(2,128)(2,1)S(1)} %copy-done.1, bf16[2,2,512]{2,1,0:T(2,128)(2,1)S(1)} %copy-done.2, bf16[8,2,256,512]{3,2,1,0:T(8,128)(2,1)S(1)} %copy-done), custom_call_target="tpu_custom_call" | custom-call | tf_op jit(solution)/shard_map/local/pallas_call | solution.py:314
  16.2 0.0 collective-permute-done.5.refs_2_
  16.2 0.0 collective-permute-done.3.refs_1_
  16.2 1.6 %collective-permute-done.1.refs_0_ = f32[72,128]{1,0:T(8,128)S(1)} collective-permute-done((f32[72,128]{1,0:T(8,128)S(1)}, f32[72,128]{1,0:T(8,128)S(1)}, u32[]{:S(2)}, u32[]{:S(2)}) %collective-permute-start.1) | collective-permute-done | bytes 36896 | tf_op jit(solution)/shard_map/ppermute | solution.py:24
  17.8 0.9 %combine.1 = bf16[2,4096]{1,0:T(2,128)(2,1)} custom-call(f32[64,128]{1,0:T(8,128)S(1)} %get-tuple-element.10.state_ref, f32[40,128]{1,0:T(8,128)S(1)} %get-tuple-element.11.bias_ref, f32[72,128]{1,0:T(8,128)S(1)} %collective-permute-done.1.refs_0_, f32[72,128]{1,0:T(8,128)S(1)} %collective-permute-done.3.refs_1_, f32[72,128]{1,0:T(8,128)S(1)} %collective-permute-done.5.refs_2_), custom_call_target="tpu_custom_call" | custom-call | tf_op jit(solution)/shard_map/combine/pallas_call | solution.py:326
  (1 shorter events, 0.0 us)
Async XLA Ops:
  0.0 0.7 %copy-start.5 = (s32[2]{0:T(128)S(1)}, s32[2]{0:T(128)}, u32[]{:S(2)}) copy-start(s32[2]{0:T(128)} %length_ref.3) | copy-start | bytes 28
  0.0 0.7 %copy-start.3 = (s32[2,4]{1,0:T(2,128)S(1)}, s32[2,4]{1,0:T(2,128)}, u32[]{:S(2)}) copy-start(s32[2,4]{1,0:T(2,128)} %owner_ref.3) | copy-start | bytes 100
  0.0 0.7 %copy-start.4 = (s32[2,4]{1,0:T(2,128)S(1)}, s32[2,4]{1,0:T(2,128)}, u32[]{:S(2)}) copy-start(s32[2,4]{1,0:T(2,128)} %places_ref.3) | copy-start | bytes 100
  0.0 0.8 %copy-start.1 = (bf16[2,4096]{1,0:T(2,128)(2,1)S(1)}, bf16[2,4096]{1,0:T(2,128)(2,1)}, u32[]{:S(2)}) copy-start(bf16[2,4096]{1,0:T(2,128)(2,1)} %queries_ref.3) | copy-start | bytes 49156
  0.8 7.4 %copy-start = (bf16[8,2,256,512]{3,2,1,0:T(8,128)(2,1)S(1)}, bf16[8,2,256,512]{3,2,1,0:T(8,128)(2,1)}, u32[]{:S(2)}) copy-start(bf16[8,2,256,512]{3,2,1,0:T(8,128)(2,1)} %pages_ref.7) | copy-start | bytes 12582916
  1.0 7.2 %collective-permute-start.4 = (bf16[72,128]{1,0:T(8,128)(2,1)S(1)}, bf16[72,128]{1,0:T(8,128)(2,1)S(1)}, u32[]{:S(2)}, u32[]{:S(2)}) collective-permute-start(bf16[72,128]{1,0:T(8,128)(2,1)S(1)} %get-tuple-element.14), channel_id=1, source_target_pairs={{0,6},{2,8},{4,10},{6,12},{8,14},{10,0},{12,2},{14,4},{1,7},{3,9},... | collective-permute-start | bytes 55304 | tf_op jit(solution)/shard_map/ppermute | solution.py:24
  5.1 6.2 %collective-permute-start.2 = (bf16[72,128]{1,0:T(8,128)(2,1)S(1)}, bf16[72,128]{1,0:T(8,128)(2,1)S(1)}, u32[]{:S(2)}, u32[]{:S(2)}) collective-permute-start(bf16[72,128]{1,0:T(8,128)(2,1)S(1)} %get-tuple-element.13), channel_id=1, source_target_pairs={{0,4},{2,6},{4,8},{6,10},{8,12},{10,14},{12,0},{14,2},{1,5},{3,7},... | collective-permute-start | bytes 55304 | tf_op jit(solution)/shard_map/ppermute | solution.py:24
  6.6 6.7 %collective-permute-start = (bf16[72,128]{1,0:T(8,128)(2,1)S(1)}, bf16[72,128]{1,0:T(8,128)(2,1)S(1)}, u32[]{:S(2)}, u32[]{:S(2)}) collective-permute-start(bf16[72,128]{1,0:T(8,128)(2,1)S(1)} %get-tuple-element.12), channel_id=1, source_target_pairs={{0,2},{2,4},{4,6},{6,8},{8,10},{10,12},{12,14},{14,0},{1,3},{3,5},... | collective-permute-start | bytes 55304 | tf_op jit(solution)/shard_map/ppermute | solution.py:24
  8.7 6.4 %copy-start.2 = (bf16[2,2,512]{2,1,0:T(2,128)(2,1)S(1)}, bf16[2,2,512]{2,1,0:T(2,128)(2,1)}, u32[]{:S(2)}) copy-start(bf16[2,2,512]{2,1,0:T(2,128)(2,1)} %fresh_ref.1) | copy-start | bytes 12292
  8.7 7.5 %collective-permute-start.5 = (f32[72,128]{1,0:T(8,128)S(1)}, f32[72,128]{1,0:T(8,128)S(1)}, u32[]{:S(2)}, u32[]{:S(2)}) collective-permute-start(f32[72,128]{1,0:T(8,128)S(1)} %attend.5), channel_id=1, source_target_pairs={{0,10},{2,12},{4,14},{6,0},{8,2},{10,4},{12,6},{14,8},{1,11},{3,13... | collective-permute-start | bytes 110600 | tf_op jit(solution)/shard_map/ppermute | solution.py:24
  11.8 4.4 %collective-permute-start.3 = (f32[72,128]{1,0:T(8,128)S(1)}, f32[72,128]{1,0:T(8,128)S(1)}, u32[]{:S(2)}, u32[]{:S(2)}) collective-permute-start(f32[72,128]{1,0:T(8,128)S(1)} %attend.4), channel_id=1, source_target_pairs={{0,12},{2,14},{4,0},{6,2},{8,4},{10,6},{12,8},{14,10},{1,13},{3,15... | collective-permute-start | bytes 110600 | tf_op jit(solution)/shard_map/ppermute | solution.py:24
  13.8 4.0 %collective-permute-start.1 = (f32[72,128]{1,0:T(8,128)S(1)}, f32[72,128]{1,0:T(8,128)S(1)}, u32[]{:S(2)}, u32[]{:S(2)}) collective-permute-start(f32[72,128]{1,0:T(8,128)S(1)} %attend.3), channel_id=1, source_target_pairs={{0,14},{2,0},{4,2},{6,4},{8,6},{10,8},{12,10},{14,12},{1,15},{3,1}... | collective-permute-start | bytes 110600 | tf_op jit(solution)/shard_map/ppermute | solution.py:24

commit v6 on v3

--- a/solution.py
+++ b/solution.py
@@ -10,7 +10,7 @@
 HEAD_DIM = 128
 REACH = 4
 TILE = 8
-PACKED_TILE = 16
+PACKED_TILE = 8
 NEVER = -1e30
 FIELD = 256
 VMEM = pl.BlockSpec(memory_space=pltpu.VMEM)
@@ -259,6 +259,7 @@
     factors = [jnp.exp(peak - highest) for peak in peaks]
     share = functools.reduce(jnp.add, [factor * total for factor, total in zip(factors, totals)])
     inverse = 1.0 / over_slots(share, jnp.add)
+    factors = [factor * inverse for factor in factors]
     for seq in range(seq_count):
         line = slice(seq, seq + 1)
         numerator = to_column(factors[0][line], 0, heads) * state_ref[seq * heads : (seq + 1) * heads, :]
@@ -266,7 +267,7 @@
             for slot in range(capacity):
                 column = to_column(factor[line], slot * heads, heads)
                 numerator = numerator + column * part[slot * heads : (slot + 1) * heads, :]
-        rows[seq * heads : (seq + 1) * heads, :] = numerator * to_column(inverse[line], 0, heads)
+        rows[seq * heads : (seq + 1) * heads, :] = numerator
     for head in range(heads):
         out_ref[:, head * HEAD_DIM : (head + 1) * HEAD_DIM] = rows[
             pl.ds(head, seq_count, stride=heads), :

time: 18.8 us -> 19 us (1.011)
  starting transfers between devices: 10.2 us -> 12.5 us
  waiting for transfers between devices: 3.97 us -> 1.72 us
    ppermute x6, starting transfers between devices: 10.2 us -> 12.5 us  [shifted(): return lax.ppermute(value, axis, pairs)]
    ppermute x6, waiting for transfers between devices: 3.97 us -> 1.72 us  [shifted(): return lax.ppermute(value, axis, pairs)]
  transfers between devices with their start and end apart: 6 -> 6, of which waited for: 3 -> 2; matrix products, arithmetic and copies ran while one was open for 0% -> 0% of each run, Pallas kernels for 14% -> 14%
where the time goes in v6:
time: 19 us; the launch traced here: 18.7 us
  starting transfers between devices  12.5 us (66%)
  Pallas kernels  3.73 us (20%)
  waiting for transfers between devices  1.72 us (9%)
  local copies, waits for them, and re-layouts  0.76 us (4%)
    ppermute x6, starting transfers between devices, shifted(): return lax.ppermute(value, axis, pairs)  12.5 us
    ppermute x6, waiting for transfers between devices, shifted(): return lax.ppermute(value, axis, pairs)  1.72 us
    pallas_call x3, Pallas kernels, body(): part = attend(payload, kv_pages)  1.46 us
    pallas_call x1, Pallas kernels, body(): pl.pallas_call(functools.partial(local_kernel, count, capacity, scale), o...  1.07 us
    pallas_call x1, Pallas kernels, body(): pl.pallas_call(functools.partial(combine_kernel, seq_count, capacity), ou...  0.93 us
    unnamed x12, local copies, waits for them, and re-layouts  0.76 us
  transfers between devices with their start and end apart: 6, of which 2 were waited for; matrix products, arithmetic and copies ran while one was open for 0% of the time, Pallas kernels for 14%

profile of v6, /device:TPU:0, one launch (start us, length us, event | category | flops | bytes accessed | tf_op | source)
XLA Modules:
  0.0 18.7 jit_solution(7009346614878702180)
XLA Ops:
  0.0 0.0 copy-start.5
  0.0 0.0 copy-start.3
  0.0 0.0 copy-start.4
  0.0 0.0 copy-start.1
  0.0 0.6 %copy-done.5 = s32[2]{0:T(128)S(1)} copy-done((s32[2]{0:T(128)S(1)}, s32[2]{0:T(128)}, u32[]{:S(2)}) %copy-start.5) | copy-done | bytes 32
  0.7 0.0 copy-done.3
  0.7 0.0 copy-done.4
  0.7 0.1 copy-done.1
  0.8 0.0 copy-start
  0.8 0.3 %pack.1 = (bf16[72,128]{1,0:T(8,128)(2,1)S(1)}, bf16[72,128]{1,0:T(8,128)(2,1)S(1)}, bf16[72,128]{1,0:T(8,128)(2,1)S(1)}) custom-call(f32[8,128]{1,0:T(8,128)S(1)} %first.1.first_ref, s32[2,4]{1,0:T(2,128)S(1)} %copy-done.3, s32[2]{0:T(128)S(1)} %copy-done.5, s32[2,4]{1,0:T(2,128)S(1)} %copy-done.4, bf16[2,4096]{1,0:T(2,128)(2,1)S(1)} %copy-done.1), custom_call_target="tpu_custom_call" | custom-call | flops 999999995904 | tf_op jit(solution)/shard_map/pack/pallas_call | solution.py:297
  1.0 4.0 %collective-permute-start.4 = (bf16[72,128]{1,0:T(8,128)(2,1)S(1)}, bf16[72,128]{1,0:T(8,128)(2,1)S(1)}, u32[]{:S(2)}, u32[]{:S(2)}) collective-permute-start(bf16[72,128]{1,0:T(8,128)(2,1)S(1)} %get-tuple-element.14), channel_id=1, source_target_pairs={{0,6},{2,8},{4,10},{6,12},{8,14},{10,0},{12,2},{14,4},{1,7},{3,9},... | collective-permute-start | bytes 55304 | tf_op jit(solution)/shard_map/ppermute | solution.py:24
  5.1 1.6 %collective-permute-start.2 = (bf16[72,128]{1,0:T(8,128)(2,1)S(1)}, bf16[72,128]{1,0:T(8,128)(2,1)S(1)}, u32[]{:S(2)}, u32[]{:S(2)}) collective-permute-start(bf16[72,128]{1,0:T(8,128)(2,1)S(1)} %get-tuple-element.13), channel_id=1, source_target_pairs={{0,4},{2,6},{4,8},{6,10},{8,12},{10,14},{12,0},{14,2},{1,5},{3,7},... | collective-permute-start | bytes 55304 | tf_op jit(solution)/shard_map/ppermute | solution.py:24
  6.6 1.5 %collective-permute-start = (bf16[72,128]{1,0:T(8,128)(2,1)S(1)}, bf16[72,128]{1,0:T(8,128)(2,1)S(1)}, u32[]{:S(2)}, u32[]{:S(2)}) collective-permute-start(bf16[72,128]{1,0:T(8,128)(2,1)S(1)} %get-tuple-element.12), channel_id=1, source_target_pairs={{0,2},{2,4},{4,6},{6,8},{8,10},{10,12},{12,14},{14,0},{1,3},{3,5},... | collective-permute-start | bytes 55304 | tf_op jit(solution)/shard_map/ppermute | solution.py:24
  8.2 0.0 collective-permute-done.4.payload_ref
  8.2 0.0 copy-done
  8.2 0.5 %attend.5 = f32[72,128]{1,0:T(8,128)S(1)} custom-call(bf16[72,128]{1,0:T(8,128)(2,1)S(1)} %collective-permute-done.4.payload_ref, bf16[8,2,256,512]{3,2,1,0:T(8,128)(2,1)S(1)} %copy-done), custom_call_target="tpu_custom_call" | custom-call | tf_op jit(solution)/shard_map/attend/pallas_call | solution.py:318
  8.7 0.0 copy-start.2
  8.7 2.6 %collective-permute-start.5 = (f32[72,128]{1,0:T(8,128)S(1)}, f32[72,128]{1,0:T(8,128)S(1)}, u32[]{:S(2)}, u32[]{:S(2)}) collective-permute-start(f32[72,128]{1,0:T(8,128)S(1)} %attend.5), channel_id=1, source_target_pairs={{0,10},{2,12},{4,14},{6,0},{8,2},{10,4},{12,6},{14,8},{1,11},{3,13... | collective-permute-start | bytes 110600 | tf_op jit(solution)/shard_map/ppermute | solution.py:24
  11.3 0.0 collective-permute-done.2.payload_ref
  11.3 0.5 %attend.4 = f32[72,128]{1,0:T(8,128)S(1)} custom-call(bf16[72,128]{1,0:T(8,128)(2,1)S(1)} %collective-permute-done.2.payload_ref, bf16[8,2,256,512]{3,2,1,0:T(8,128)(2,1)S(1)} %copy-done), custom_call_target="tpu_custom_call" | custom-call | tf_op jit(solution)/shard_map/attend/pallas_call | solution.py:318
  11.8 1.4 %collective-permute-start.3 = (f32[72,128]{1,0:T(8,128)S(1)}, f32[72,128]{1,0:T(8,128)S(1)}, u32[]{:S(2)}, u32[]{:S(2)}) collective-permute-start(f32[72,128]{1,0:T(8,128)S(1)} %attend.4), channel_id=1, source_target_pairs={{0,12},{2,14},{4,0},{6,2},{8,4},{10,6},{12,8},{14,10},{1,13},{3,15... | collective-permute-start | bytes 110600 | tf_op jit(solution)/shard_map/ppermute | solution.py:24
  13.2 0.1 collective-permute-done.payload_ref
  13.3 0.5 %attend.3 = f32[72,128]{1,0:T(8,128)S(1)} custom-call(bf16[72,128]{1,0:T(8,128)(2,1)S(1)} %collective-permute-done.payload_ref, bf16[8,2,256,512]{3,2,1,0:T(8,128)(2,1)S(1)} %copy-done), custom_call_target="tpu_custom_call" | custom-call | tf_op jit(solution)/shard_map/attend/pallas_call | solution.py:318
  13.8 1.3 %collective-permute-start.1 = (f32[72,128]{1,0:T(8,128)S(1)}, f32[72,128]{1,0:T(8,128)S(1)}, u32[]{:S(2)}, u32[]{:S(2)}) collective-permute-start(f32[72,128]{1,0:T(8,128)S(1)} %attend.3), channel_id=1, source_target_pairs={{0,14},{2,0},{4,2},{6,4},{8,6},{10,8},{12,10},{14,12},{1,15},{3,1}... | collective-permute-start | bytes 110600 | tf_op jit(solution)/shard_map/ppermute | solution.py:24
  15.1 0.0 copy-done.2
  15.1 1.1 %local.1 = (f32[64,128]{1,0:T(8,128)S(1)}, f32[40,128]{1,0:T(8,128)S(1)}) custom-call(s32[2,4]{1,0:T(2,128)S(1)} %copy-done.3, s32[2]{0:T(128)S(1)} %copy-done.5, s32[2,4]{1,0:T(2,128)S(1)} %copy-done.4, bf16[2,4096]{1,0:T(2,128)(2,1)S(1)} %copy-done.1, bf16[2,2,512]{2,1,0:T(2,128)(2,1)S(1)} %copy-done.2, bf16[8,2,256,512]{3,2,1,0:T(8,128)(2,1)S(1)} %copy-done), custom_call_target="tpu_custom_call" | custom-call | tf_op jit(solution)/shard_map/local/pallas_call | solution.py:320
  16.2 0.0 collective-permute-done.5.refs_2_
  16.2 0.0 collective-permute-done.3.refs_1_
  16.2 1.6 %collective-permute-done.1.refs_0_ = f32[72,128]{1,0:T(8,128)S(1)} collective-permute-done((f32[72,128]{1,0:T(8,128)S(1)}, f32[72,128]{1,0:T(8,128)S(1)}, u32[]{:S(2)}, u32[]{:S(2)}) %collective-permute-start.1) | collective-permute-done | bytes 36896 | tf_op jit(solution)/shard_map/ppermute | solution.py:24
  17.8 0.9 %combine.1 = bf16[2,4096]{1,0:T(2,128)(2,1)} custom-call(f32[64,128]{1,0:T(8,128)S(1)} %get-tuple-element.10.state_ref, f32[40,128]{1,0:T(8,128)S(1)} %get-tuple-element.11.bias_ref, f32[72,128]{1,0:T(8,128)S(1)} %collective-permute-done.1.refs_0_, f32[72,128]{1,0:T(8,128)S(1)} %collective-permute-done.3.refs_1_, f32[72,128]{1,0:T(8,128)S(1)} %collective-permute-done.5.refs_2_), custom_call_target="tpu_custom_call" | custom-call | tf_op jit(solution)/shard_map/combine/pallas_call | solution.py:332
  (1 shorter events, 0.0 us)
Async XLA Ops:
  0.0 0.7 %copy-start.5 = (s32[2]{0:T(128)S(1)}, s32[2]{0:T(128)}, u32[]{:S(2)}) copy-start(s32[2]{0:T(128)} %length_ref.3) | copy-start | bytes 28
  0.0 0.7 %copy-start.3 = (s32[2,4]{1,0:T(2,128)S(1)}, s32[2,4]{1,0:T(2,128)}, u32[]{:S(2)}) copy-start(s32[2,4]{1,0:T(2,128)} %owner_ref.3) | copy-start | bytes 100
  0.0 0.7 %copy-start.4 = (s32[2,4]{1,0:T(2,128)S(1)}, s32[2,4]{1,0:T(2,128)}, u32[]{:S(2)}) copy-start(s32[2,4]{1,0:T(2,128)} %places_ref.3) | copy-start | bytes 100
  0.0 0.8 %copy-start.1 = (bf16[2,4096]{1,0:T(2,128)(2,1)S(1)}, bf16[2,4096]{1,0:T(2,128)(2,1)}, u32[]{:S(2)}) copy-start(bf16[2,4096]{1,0:T(2,128)(2,1)} %queries_ref.3) | copy-start | bytes 49156
  0.8 7.4 %copy-start = (bf16[8,2,256,512]{3,2,1,0:T(8,128)(2,1)S(1)}, bf16[8,2,256,512]{3,2,1,0:T(8,128)(2,1)}, u32[]{:S(2)}) copy-start(bf16[8,2,256,512]{3,2,1,0:T(8,128)(2,1)} %pages_ref.7) | copy-start | bytes 12582916
  1.0 7.2 %collective-permute-start.4 = (bf16[72,128]{1,0:T(8,128)(2,1)S(1)}, bf16[72,128]{1,0:T(8,128)(2,1)S(1)}, u32[]{:S(2)}, u32[]{:S(2)}) collective-permute-start(bf16[72,128]{1,0:T(8,128)(2,1)S(1)} %get-tuple-element.14), channel_id=1, source_target_pairs={{0,6},{2,8},{4,10},{6,12},{8,14},{10,0},{12,2},{14,4},{1,7},{3,9},... | collective-permute-start | bytes 55304 | tf_op jit(solution)/shard_map/ppermute | solution.py:24
  5.1 6.2 %collective-permute-start.2 = (bf16[72,128]{1,0:T(8,128)(2,1)S(1)}, bf16[72,128]{1,0:T(8,128)(2,1)S(1)}, u32[]{:S(2)}, u32[]{:S(2)}) collective-permute-start(bf16[72,128]{1,0:T(8,128)(2,1)S(1)} %get-tuple-element.13), channel_id=1, source_target_pairs={{0,4},{2,6},{4,8},{6,10},{8,12},{10,14},{12,0},{14,2},{1,5},{3,7},... | collective-permute-start | bytes 55304 | tf_op jit(solution)/shard_map/ppermute | solution.py:24
  6.6 6.7 %collective-permute-start = (bf16[72,128]{1,0:T(8,128)(2,1)S(1)}, bf16[72,128]{1,0:T(8,128)(2,1)S(1)}, u32[]{:S(2)}, u32[]{:S(2)}) collective-permute-start(bf16[72,128]{1,0:T(8,128)(2,1)S(1)} %get-tuple-element.12), channel_id=1, source_target_pairs={{0,2},{2,4},{4,6},{6,8},{8,10},{10,12},{12,14},{14,0},{1,3},{3,5},... | collective-permute-start | bytes 55304 | tf_op jit(solution)/shard_map/ppermute | solution.py:24
  8.7 6.4 %copy-start.2 = (bf16[2,2,512]{2,1,0:T(2,128)(2,1)S(1)}, bf16[2,2,512]{2,1,0:T(2,128)(2,1)}, u32[]{:S(2)}) copy-start(bf16[2,2,512]{2,1,0:T(2,128)(2,1)} %fresh_ref.1) | copy-start | bytes 12292
  8.7 7.5 %collective-permute-start.5 = (f32[72,128]{1,0:T(8,128)S(1)}, f32[72,128]{1,0:T(8,128)S(1)}, u32[]{:S(2)}, u32[]{:S(2)}) collective-permute-start(f32[72,128]{1,0:T(8,128)S(1)} %attend.5), channel_id=1, source_target_pairs={{0,10},{2,12},{4,14},{6,0},{8,2},{10,4},{12,6},{14,8},{1,11},{3,13... | collective-permute-start | bytes 110600 | tf_op jit(solution)/shard_map/ppermute | solution.py:24
  11.8 4.4 %collective-permute-start.3 = (f32[72,128]{1,0:T(8,128)S(1)}, f32[72,128]{1,0:T(8,128)S(1)}, u32[]{:S(2)}, u32[]{:S(2)}) collective-permute-start(f32[72,128]{1,0:T(8,128)S(1)} %attend.4), channel_id=1, source_target_pairs={{0,12},{2,14},{4,0},{6,2},{8,4},{10,6},{12,8},{14,10},{1,13},{3,15... | collective-permute-start | bytes 110600 | tf_op jit(solution)/shard_map/ppermute | solution.py:24
  13.8 4.0 %collective-permute-start.1 = (f32[72,128]{1,0:T(8,128)S(1)}, f32[72,128]{1,0:T(8,128)S(1)}, u32[]{:S(2)}, u32[]{:S(2)}) collective-permute-start(f32[72,128]{1,0:T(8,128)S(1)} %attend.3), channel_id=1, source_target_pairs={{0,14},{2,0},{4,2},{6,4},{8,6},{10,8},{12,10},{14,12},{1,15},{3,1}... | collective-permute-start | bytes 110600 | tf_op jit(solution)/shard_map/ppermute | solution.py:24
